TPU v7x, 512 devices: a whole 4x8x8 slice. The times are simulated.
512 devices in a mesh: row: 16 (over z, x_lo), col: 32 (over x_hi, y, core).
Axes of the slice: x: 4 (x_hi: 2, x_lo: 2; x = x_hi * 2 + x_lo), y: 8, z: 8, core: 2. Of those that a mesh axis runs over, the one named last changes fastest.
Arguments:
- tokens: bfloat16 [2048, 4096], P('row', 'col'), may hold values from -6 to 6
- upstream: bfloat16 [2048, 4096], P('row', 'col'), may hold values from -6 to 6
- w_in: bfloat16 [32, 16, 256, 256], P('col', 'row'), may hold values from -0.1875 to 0.1875
- in_codes: int32 [32, 16], P('col'), may hold values from -1 to 31, as said below
- w_out: bfloat16 [32, 16, 256, 256], P('col', 'row'), may hold values from -0.09375 to 0.09375
- out_codes: int32 [32, 16], P('col'), may hold values from -1 to 31, as said below
Outputs:
- layer_out: bfloat16 [2048, 4096], P('row', 'col')
- grad_tokens: bfloat16 [2048, 4096], P('row', 'col')
- grad_w_in: bfloat16 [32, 16, 256, 256], P('col', 'row')
- grad_w_out: bfloat16 [32, 16, 256, 256], P('col', 'row')
Inputs may be any that keep to these rules, and one draw needn't show every extreme that they name: `in_codes`: row c describes panel c's 16 slots: a code k names input tile row k // 2 and local hidden tile column k % 2; -1 marks an empty slot. Codes of a row are distinct, every row has one filled slot or more, and some row has all 16 slots filled. `out_codes`: row c describes panel c's 16 slots: a code k names output tile column k // 2 and local hidden tile row k % 2; -1 marks an empty slot. Codes of a row are distinct, every row has one filled slot or more, and some row has all 16 slots filled.
All inputs are finite; a program needn't handle non-finite values.
Results may differ from a plain program's by a relative error of at most 0.015.
Values may be sent and summed in bfloat16 or wider, within the bound.
A program may use at most 64 MiB of HBM per device.

v0:
```python
import jax
import jax.numpy as jnp
from jax import lax
from jax.sharding import PartitionSpec as P

D = 4096
FF = 16384


def silu_slope(hidden):
    sigmoid_value = jax.nn.sigmoid(hidden)
    return sigmoid_value * (1.0 + hidden * (1.0 - sigmoid_value))


def split_codes(slot_codes, tile_cols):
    filled = slot_codes >= 0
    clipped = jnp.maximum(slot_codes, 0)
    return (clipped // tile_cols, clipped % tile_cols, filled)


def selector(position, filled, classes):
    matches = position[:, None] == jnp.arange(classes, dtype=jnp.int32)[None, :]
    return (matches & filled[:, None]).astype(jnp.float32)


def slices_at(row_codes, col_codes, filled):
    return (row_codes, col_codes, filled)


def per_device(tokens, upstream, w_in, in_codes, w_out, out_codes):
    tile_size = w_in.shape[3]
    row_count = tokens.shape[0]
    tile_rows = D // tile_size
    tile_cols = FF // (tile_size * lax.axis_size("col"))
    own_slots = w_in.shape[1]
    highest = lax.Precision.HIGHEST
    in_row, in_col, in_filled = split_codes(in_codes[0], tile_cols)
    out_row, out_col, out_filled = split_codes(out_codes[0], tile_cols)
    first_slot = lax.axis_index("row") * own_slots
    whole_tokens, whole_upstream = (
        lax.all_gather(tokens, "col", axis=1, tiled=True),
        lax.all_gather(upstream, "col", axis=1, tiled=True),
    )
    token_tiles = whole_tokens.reshape(row_count, tile_rows, tile_size)
    up_tiles = whole_upstream.reshape(row_count, tile_rows, tile_size)
    slot_major_tokens = jnp.swapaxes(token_tiles, 0, 1)
    rows_at, cols_at, filled_at = slices_at(in_row, in_col, in_filled)
    picked = jnp.take(token_tiles, rows_at, axis=1)
    partial_sum = jnp.einsum(
        "tkd,kdn->tkn",
        picked,
        lax.all_gather(w_in, "row", axis=1, tiled=True)[0],
        preferred_element_type=jnp.float32,
    )
    hidden = jnp.einsum(
        "tkn,kj->tjn", partial_sum, selector(cols_at, filled_at, tile_cols), precision=highest
    )
    activ = jax.nn.silu(hidden).astype(jnp.bfloat16)
    rows_at, cols_at, filled_at = slices_at(out_row, out_col, out_filled)
    picked = jnp.take(activ, cols_at, axis=1)
    partial_sum = jnp.einsum(
        "tkf,kfd->tkd",
        picked,
        lax.all_gather(w_out, "row", axis=1, tiled=True)[0],
        preferred_element_type=jnp.float32,
    )
    layer_part = jnp.einsum(
        "tkd,ki->tid", partial_sum, selector(rows_at, filled_at, tile_rows), precision=highest
    )
    layer_out = lax.psum_scatter(
        layer_part.reshape(row_count, D).astype(jnp.bfloat16),
        "col",
        scatter_dimension=1,
        tiled=True,
    )
    rows_at, cols_at, filled_at = slices_at(out_row, out_col, out_filled)
    picked = jnp.take(up_tiles, rows_at, axis=1)
    partial_sum = jnp.einsum(
        "tkd,kfd->tkf",
        picked,
        lax.all_gather(w_out, "row", axis=1, tiled=True)[0],
        preferred_element_type=jnp.float32,
    )
    grad_activ = jnp.einsum(
        "tkf,kj->tjf", partial_sum, selector(cols_at, filled_at, tile_cols), precision=highest
    )
    grad_hidden = (grad_activ * silu_slope(hidden)).astype(jnp.bfloat16)
    grad_sends = jnp.take(jnp.swapaxes(grad_hidden, 0, 1), in_col, axis=0)
    activ_sends = jnp.take(jnp.swapaxes(activ, 0, 1), out_col, axis=0)
    upstream_sends = jnp.take(jnp.swapaxes(up_tiles, 0, 1), out_row, axis=0)
    token_sends = jnp.take(slot_major_tokens, in_row, axis=0)
    token_slots, grad_slots, activ_slots, upstream_slots = (
        lax.all_to_all(token_sends, "row", split_axis=0, concat_axis=1, tiled=True),
        lax.all_to_all(grad_sends, "row", split_axis=0, concat_axis=1, tiled=True),
        lax.all_to_all(activ_sends, "row", split_axis=0, concat_axis=1, tiled=True),
        lax.all_to_all(upstream_sends, "row", split_axis=0, concat_axis=1, tiled=True),
    )
    rows_at, cols_at, filled_at = slices_at(in_row, in_col, in_filled)
    picked = jnp.take(grad_hidden, cols_at, axis=1)
    partial_sum = jnp.einsum(
        "tkf,kdf->tkd",
        picked,
        lax.all_gather(w_in, "row", axis=1, tiled=True)[0],
        preferred_element_type=jnp.float32,
    )
    input_part = jnp.einsum(
        "tkd,ki->tid", partial_sum, selector(rows_at, filled_at, tile_rows), precision=highest
    )
    grad_tokens = lax.psum_scatter(
        input_part.reshape(row_count, D).astype(jnp.bfloat16),
        "col",
        scatter_dimension=1,
        tiled=True,
    )
    mine_in = lax.dynamic_slice_in_dim(in_filled, first_slot, own_slots)
    mine_out = lax.dynamic_slice_in_dim(out_filled, first_slot, own_slots)
    grad_w_in = jnp.einsum(
        "ktd,ktn->kdn", token_slots, grad_slots, preferred_element_type=jnp.float32
    )
    grad_w_in = jnp.where(mine_in[:, None, None], grad_w_in, 0.0).astype(jnp.bfloat16)[None]
    grad_w_out = jnp.einsum(
        "ktf,ktd->kfd", activ_slots, upstream_slots, preferred_element_type=jnp.float32
    )
    grad_w_out = jnp.where(mine_out[:, None, None], grad_w_out, 0.0).astype(jnp.bfloat16)[None]
    return (layer_out, grad_tokens, grad_w_in, grad_w_out)


def solution(mesh):
    placed = (
        P("row", "col"),
        P("row", "col"),
        P("col", "row", None, None),
        P("col", None),
        P("col", "row", None, None),
        P("col", None),
    )
    return jax.shard_map(
        per_device,
        mesh=mesh,
        in_specs=placed,
        out_specs=(
            P("row", "col"),
            P("row", "col"),
            P("col", "row", None, None),
            P("col", "row", None, None),
        ),
        check_vma=False,
    )
```

profile of v0, /device:TPU:1, one launch (start us, length us, event | category | flops | bytes accessed | tf_op | source)
XLA Modules:
  0.0 626.7 jit_solution(14606275297330410834)
XLA Ops:
  7.2 0.0 all-gather.11.cloned.1.call-start
  7.2 1.5 copy.59
  8.7 0.0 all-gather.11.cloned.1.call-update
  8.7 0.0 all-gather.5.cloned.1.call-start
  8.8 1.5 copy.52
  10.2 0.0 all-gather.5.cloned.1.call-update
  10.3 0.0 all-gather.9.cloned.1.call-start
  10.3 0.7 all-gather.9.cloned.1.call-update
  11.0 0.0 all-gather.7.cloned.1.call-start
  11.0 0.5 all-gather.7.cloned.1.call-update
  11.6 0.7 compare_and_fusion.1
  12.3 88.4 %all-gather.11.cloned.1.call-done = bf16[128,4096]{0,1:T(8,128)(2,1)} async-done(((bf16[128,128]{0,1:T(8,128)(2,1)}), bf16[128,4096]{0,1:T(8,128)(2,1)}) %all-gather.11.cloned.1.call-update) | async-done | bytes 1048592 | tf_op jit(solution)/shard_map/all_gather | solution.py:42
  100.7 1.5 copy.60
  102.2 0.6 gather_fusion.7
  102.9 1.1 broadcast_select_fusion.3
  104.0 7.3 %all-to-all-start.3 = ((bf16[16,128,256]{2,1,0:T(8,128)(2,1)}), bf16[16,128,256]{2,1,0:T(8,128)(2,1)}, u32[]{:S(2)}, u32[]{:S(2)}) async-start(bf16[16,128,256]{2,1,0:T(8,128)(2,1)} %broadcast_select_fusion.3), calls=%async_computation.3 | async-start | bytes 2097152 | tf_op jit(solution)/shard_map/all_to_all | solution.py:96
  111.3 0.5 broadcast_compare_fusion
  111.8 0.5 broadcast_compare_fusion.1
  112.4 72.2 %all-gather.5.cloned.1.call-done = bf16[128,4096]{0,1:T(8,128)(2,1)} async-done(((bf16[128,128]{0,1:T(8,128)(2,1)}), bf16[128,4096]{0,1:T(8,128)(2,1)}) %all-gather.5.cloned.1.call-update) | async-done | bytes 1048592 | tf_op jit(solution)/shard_map/all_gather | solution.py:41
  184.6 1.5 copy.53
  186.1 1.6 gather_fusion.4
  187.7 1.6 copy.65
  189.3 1.1 broadcast_select_fusion.1
  190.5 7.3 %all-to-all-start = ((bf16[16,128,256]{1,2,0:T(8,128)(2,1)}), bf16[16,128,256]{1,2,0:T(8,128)(2,1)}, u32[]{:S(2)}, u32[]{:S(2)}) async-start(bf16[16,128,256]{1,2,0:T(8,128)(2,1)} %broadcast_select_fusion.1), calls=%async_computation | async-start | bytes 2097152 | tf_op jit(solution)/shard_map/all_to_all | solution.py:93
  197.8 0.6 gather_fusion.2
  198.4 0.6 gather_fusion
  199.0 66.5 %all-gather.9.cloned.1.call-done = bf16[1,16,256,256]{3,2,0,1:T(8,128)(2,1)} async-done(((bf16[1,1,256,256]{3,2,0,1:T(8,128)(2,1)}), bf16[1,16,256,256]{3,2,0,1:T(8,128)(2,1)}) %all-gather.9.cloned.1.call-update) | async-done | bytes 2097168 | tf_op jit(solution)/shard_map/all_gather | solution.py:64
  265.5 2.4 fusion.25
  267.9 2.0 fusion.10
  269.9 69.4 %all-gather.7.cloned.1.call-done = bf16[1,16,256,256]{3,2,0,1:T(8,128)(2,1)} async-done(((bf16[1,1,256,256]{3,2,0,1:T(8,128)(2,1)}), bf16[1,16,256,256]{3,2,0,1:T(8,128)(2,1)}) %all-gather.7.cloned.1.call-update) | async-done | bytes 2097168 | tf_op jit(solution)/shard_map/all_gather | solution.py:52
  339.3 2.1 fusion.16
  341.5 2.0 fusion.14
  343.4 0.1 multiply_convert_fusion
  343.6 0.6 gather_fusion.6
  344.2 0.7 copy.70
  344.9 1.2 broadcast_select_fusion
  346.1 5.5 all-to-all-start.2
  351.6 0.2 reduce-scatter.7.cloned.1.call-start
  351.9 0.1 fusion.62
  352.0 0.6 gather_fusion.1
  352.6 0.5 fusion.22
  353.2 0.1 copy-done.5
  353.3 2.3 fusion.37
  355.6 1.7 copy.76
  357.3 0.0 reduce-scatter.7.cloned.1.call-update
  357.4 1.6 gather_fusion.3
  359.0 0.6 gather_fusion.5
  359.6 1.2 broadcast_select_fusion.2
  360.8 0.5 copy-done.3
  361.3 2.2 fusion.19
  363.5 6.2 all-to-all-done.2
  369.7 6.5 %all-to-all-start.1 = ((bf16[16,128,256]{2,1,0:T(8,128)(2,1)}), bf16[16,128,256]{2,1,0:T(8,128)(2,1)}, u32[]{:S(2)}, u32[]{:S(2)}) async-start(bf16[16,128,256]{2,1,0:T(8,128)(2,1)} %broadcast_select_fusion.2), calls=%async_computation.1 | async-start | bytes 2097152 | tf_op jit(solution)/shard_map/all_to_all | solution.py:94
  376.2 0.0 reduce-scatter.9.cloned.1.call-start
  376.2 2.3 fusion.34
  378.6 1.8 copy.77
  380.3 0.0 reduce-scatter.9.cloned.1.call-update
  380.3 0.6 constant_dynamic-slice_fusion.1
  381.0 0.6 constant_dynamic-slice_fusion
  381.6 103.2 %reduce-scatter.7.cloned.1.call-done = bf16[128,128]{1,0:T(8,128)(2,1)} async-done(((bf16[4096,128]{1,0:T(8,128)(2,1)}), bf16[128,128]{1,0:T(8,128)(2,1)}) %reduce-scatter.7.cloned.1.call-update) | async-done | bytes 32784
  484.7 1.5 copy.73
  486.2 125.6 %reduce-scatter.9.cloned.1.call-done = bf16[128,128]{1,0:T(8,128)(2,1)} async-done(((bf16[4096,128]{1,0:T(8,128)(2,1)}), bf16[128,128]{1,0:T(8,128)(2,1)}) %reduce-scatter.9.cloned.1.call-update) | async-done | bytes 32784
  611.8 1.5 copy.75
  613.3 3.3 fusion.45
  616.6 3.2 fusion.44
  (42 shorter events, 0.1 us)
Async XLA Ops:
  7.2 93.5 %all-gather.11.cloned.1.call-start = ((), (), s32[]{:S(2)}) async-start(), calls=%async_computation.9 | async-start | bytes 1081344 | tf_op jit(solution)/shard_map/all_gather | solution.py:42
  8.7 175.9 %all-gather.5.cloned.1.call-start = ((), (), s32[]{:S(2)}) async-start(), calls=%async_computation.6 | async-start | bytes 1081344 | tf_op jit(solution)/shard_map/all_gather | solution.py:41
  10.3 255.2 %all-gather.9.cloned.1.call-start = ((), (), s32[]{:S(2)}) async-start(), calls=%async_computation.8 | async-start | bytes 2228224 | tf_op jit(solution)/shard_map/all_gather | solution.py:64
  11.0 328.3 %all-gather.7.cloned.1.call-start = ((), (), s32[]{:S(2)}) async-start(), calls=%async_computation.7 | async-start | bytes 2228224 | tf_op jit(solution)/shard_map/all_gather | solution.py:52
  12.2 90.6 %copy-start.4 = (s32[16]{0:T(128)}, s32[16]{0:T(128)S(1)}, u32[]{:S(2)}) copy-start(s32[16]{0:T(128)S(1)} %get-tuple-element.11) | copy-start | bytes 196
  102.8 8.4 %copy-start.12 = (s32[1,16]{1,0:T(1,128)S(1)}, s32[1,16]{1,0:T(1,128)}, u32[]{:S(2)}) copy-start(s32[1,16]{1,0:T(1,128)} %param.17) | copy-start | bytes 196
  102.8 9.0 %copy-start.13 = (s32[1,16]{1,0:T(1,128)S(1)}, s32[1,16]{1,0:T(1,128)}, u32[]{:S(2)}) copy-start(s32[1,16]{1,0:T(1,128)} %param.19) | copy-start | bytes 196
  104.0 86.5 %all-to-all-start.3 = ((bf16[16,128,256]{2,1,0:T(8,128)(2,1)}), bf16[16,128,256]{2,1,0:T(8,128)(2,1)}, u32[]{:S(2)}, u32[]{:S(2)}) async-start(bf16[16,128,256]{2,1,0:T(8,128)(2,1)} %broadcast_select_fusion.3), calls=%async_computation.3 | async-start | bytes 2097152 | tf_op jit(solution)/shard_map/all_to_all | solution.py:96
  111.3 230.1 %copy-start.10 = (s32[16]{0:T(128)}, s32[16]{0:T(128)S(1)}, u32[]{:S(2)}) copy-start(s32[16]{0:T(128)S(1)} %get-tuple-element.9) | copy-start | bytes 196
  111.8 229.6 %copy-start.6 = (pred[16]{0:T(512)(128)(4,1)}, pred[16]{0:T(512)(128)(4,1)S(1)}, u32[]{:S(2)}) copy-start(pred[16]{0:T(512)(128)(4,1)S(1)} %get-tuple-element.23) | copy-start | bytes 52
  112.4 155.5 %copy-start.8 = (pred[16]{0:T(512)(128)(4,1)}, pred[16]{0:T(512)(128)(4,1)S(1)}, u32[]{:S(2)}) copy-start(pred[16]{0:T(512)(128)(4,1)S(1)} %get-tuple-element.21) | copy-start | bytes 52
  190.5 155.6 %all-to-all-start = ((bf16[16,128,256]{1,2,0:T(8,128)(2,1)}), bf16[16,128,256]{1,2,0:T(8,128)(2,1)}, u32[]{:S(2)}, u32[]{:S(2)}) async-start(bf16[16,128,256]{1,2,0:T(8,128)(2,1)} %broadcast_select_fusion.1), calls=%async_computation | async-start | bytes 2097152 | tf_op jit(solution)/shard_map/all_to_all | solution.py:93
  346.1 6.5 %copy-start.1 = (bf16[1,16,256,256]{3,2,0,1:T(8,128)(2,1)S(1)}, bf16[1,16,256,256]{3,2,0,1:T(8,128)(2,1)}, u32[]{:S(2)}) copy-start(bf16[1,16,256,256]{3,2,0,1:T(8,128)(2,1)} %all-gather.9.cloned.1.call-done) | copy-start | bytes 6291460
  346.1 23.6 %all-to-all-start.2 = ((bf16[16,128,256]{1,2,0:T(8,128)(2,1)}), bf16[16,128,256]{1,2,0:T(8,128)(2,1)}, u32[]{:S(2)}, u32[]{:S(2)}) async-start(bf16[16,128,256]{1,2,0:T(8,128)(2,1)} %broadcast_select_fusion), calls=%async_computation.2 | async-start | bytes 2097152 | tf_op jit(solution)/shard_map/all_to_all | solution.py:95
  351.6 133.1 %reduce-scatter.7.cloned.1.call-start = ((), (), s32[]{:S(2)}) async-start(), calls=%async_computation.10 | async-start | bytes 1081344
  352.6 0.7 copy-start.5
  352.6 0.6 copy-start.9
  355.6 1.8 copy-start.11
  359.0 1.8 copy-start
  359.6 1.7 copy-start.3
  361.3 14.9 %copy-start.7 = (pred[16]{0:T(512)(128)(4,1)S(1)}, pred[16]{0:T(512)(128)(4,1)}, u32[]{:S(2)}) copy-start(pred[16]{0:T(512)(128)(4,1)} %copy-done.6) | copy-start | bytes 52
  363.5 12.7 %copy-start.2 = (f32[128,16,256]{2,0,1:T(8,128)S(1)}, f32[128,16,256]{2,0,1:T(8,128)}, u32[]{:S(2)}) copy-start(f32[128,16,256]{2,0,1:T(8,128)} %fusion.19) | copy-start | bytes 6291460
  369.7 246.9 %all-to-all-start.1 = ((bf16[16,128,256]{2,1,0:T(8,128)(2,1)}), bf16[16,128,256]{2,1,0:T(8,128)(2,1)}, u32[]{:S(2)}, u32[]{:S(2)}) async-start(bf16[16,128,256]{2,1,0:T(8,128)(2,1)} %broadcast_select_fusion.2), calls=%async_computation.1 | async-start | bytes 2097152 | tf_op jit(solution)/shard_map/all_to_all | solution.py:94
  376.2 235.7 %reduce-scatter.9.cloned.1.call-start = ((), (), s32[]{:S(2)}) async-start(), calls=%async_computation.11 | async-start | bytes 1081344
  378.5 1.8 copy-start.14
  378.5 2.4 copy-start.15
Sparse Core Ops, SparseCore 0:
  11.9 88.7 all-gather.10
  104.6 79.9 all-gather.4
  186.7 78.7 all-gather.8
  267.4 71.8 all-gather.6
  357.5 127.2 reduce-scatter.6
  489.9 121.8 reduce-scatter.8
where the time goes:
time: 632 us; the launch traced here: 627 us
  waiting for transfers between devices  533 us (84%)
  starting transfers between devices  26.9 us (4%)
  local copies, waits for them, and re-layouts  23.4 us (4%)
  matrix products  22.3 us (4%)
  between operations  14.5 us (2%)
  other arithmetic  6.7 us (1%)
    unnamed x8, waiting for transfers between devices  230 us
    all_gather x1, waiting for transfers between devices, per_device(): lax.all_gather(upstream, 'col', axis=1, tiled=True)  88.4 us
    all_gather x1, waiting for transfers between devices, per_device(): lax.all_gather(tokens, 'col', axis=1, tiled=True)  72.2 us
    all_gather x1, waiting for transfers between devices, per_device(): lax.all_gather(w_in, 'row', axis=1, tiled=True)[0]  69.4 us
    all_gather x1, waiting for transfers between devices, per_device(): lax.all_gather(w_out, 'row', axis=1, tiled=True)[0]  66.5 us
  transfers between devices with their start and end apart: 10, of which 7 were waited for; matrix products, arithmetic and copies ran while one was open for 7% of the time, Pallas kernels for 0%

commit v1 on v0

v1 whole, which is shorter than its diff:
```python
import jax
import jax.numpy as jnp
from jax import lax
from jax.sharding import PartitionSpec as P

D = 4096
FF = 16384


def silu_slope(hidden):
    sigmoid_value = jax.nn.sigmoid(hidden)
    return sigmoid_value * (1.0 + hidden * (1.0 - sigmoid_value))


def split_codes(slot_codes, tile_cols):
    filled = slot_codes >= 0
    clipped = jnp.maximum(slot_codes, 0)
    return (clipped // tile_cols, clipped % tile_cols, filled)


def selector(position, filled, classes):
    matches = position[:, None] == jnp.arange(classes, dtype=jnp.int32)[None, :]
    return matches & filled[:, None]


def exchange(blocks, axis):
    return lax.all_to_all(blocks, axis, split_axis=0, concat_axis=0, tiled=True)


def gathered(block, axis):
    copies = jnp.broadcast_to(block[None], (lax.axis_size(axis), *block.shape))
    return exchange(copies, axis)


def tile_major(blocks, tile_size):
    n, rows, width = blocks.shape
    per_tile = tile_size // width
    tiles = blocks.reshape(n // per_tile, per_tile, rows, width)
    return jnp.swapaxes(tiles, 1, 2).reshape(n // per_tile, rows, tile_size)


def col_summed(parts, cols):
    tiles, rows, tile_size = parts.shape
    width = tiles * tile_size // cols
    per_tile = tile_size // width
    blocks = jnp.swapaxes(parts.reshape(tiles, rows, per_tile, width), 1, 2)
    blocks = exchange(blocks.reshape(cols, rows, width), "col")
    return jnp.sum(blocks.astype(jnp.float32), axis=0).astype(jnp.bfloat16)


def per_device(tokens, upstream, w_in, in_codes, w_out, out_codes):
    tile_size = w_in.shape[3]
    cols, rows = lax.axis_size("col"), lax.axis_size("row")
    tile_rows = D // tile_size
    tile_cols = FF // (tile_size * cols)
    row = lax.axis_index("row")
    in_row, in_col, in_filled = split_codes(in_codes[0], tile_cols)
    out_row, out_col, out_filled = split_codes(out_codes[0], tile_cols)
    in_j = selector(in_col, in_filled, tile_cols).astype(jnp.float32)
    out_j = selector(out_col, out_filled, tile_cols).astype(jnp.float32)
    in_i = selector(in_row, in_filled, tile_rows).astype(jnp.float32)
    out_i = selector(out_row, out_filled, tile_rows).astype(jnp.float32)
    highest = lax.Precision.HIGHEST
    f32 = jnp.float32

    token_tiles = tile_major(gathered(tokens, "col"), tile_size)
    tiles_in = gathered(w_in[0, 0], "row")
    up_tiles = tile_major(gathered(upstream, "col"), tile_size)
    tiles_out = gathered(w_out[0, 0], "row")

    picked_tokens = jnp.take(token_tiles, in_row, axis=0)
    picked_up = jnp.take(up_tiles, out_row, axis=0)
    token_slots = exchange(picked_tokens, "row")
    upstream_slots = exchange(picked_up, "row")

    products = jnp.einsum("ktd,kdn->ktn", picked_tokens, tiles_in, preferred_element_type=f32)
    hidden = jnp.sum(products[:, None] * in_j[:, :, None, None], axis=0)
    activ = jax.nn.silu(hidden).astype(jnp.bfloat16)
    picked_activ = jnp.take(activ, out_col, axis=0)
    activ_slots = exchange(picked_activ, "row")

    products = jnp.einsum("ktf,kfd->ktd", picked_activ, tiles_out, preferred_element_type=f32)
    layer_part = jnp.einsum("ktd,ki->itd", products, out_i, precision=highest)
    layer_out = col_summed(layer_part.astype(jnp.bfloat16), cols)

    products = jnp.einsum("ktd,kfd->ktf", picked_up, tiles_out, preferred_element_type=f32)
    grad_activ = jnp.sum(products[:, None] * out_j[:, :, None, None], axis=0)
    grad_hidden = (grad_activ * silu_slope(hidden)).astype(jnp.bfloat16)
    picked_grad = jnp.take(grad_hidden, in_col, axis=0)
    grad_slots = exchange(picked_grad, "row")

    products = jnp.einsum("ktf,kdf->ktd", picked_grad, tiles_in, preferred_element_type=f32)
    input_part = jnp.einsum("ktd,ki->itd", products, in_i, precision=highest)
    grad_tokens = col_summed(input_part.astype(jnp.bfloat16), cols)

    mine_in = lax.dynamic_index_in_dim(in_filled, row, keepdims=False)
    mine_out = lax.dynamic_index_in_dim(out_filled, row, keepdims=False)
    grad_w_in = jnp.einsum("rtd,rtn->dn", token_slots, grad_slots, preferred_element_type=f32)
    grad_w_in = jnp.where(mine_in, grad_w_in, 0.0).astype(jnp.bfloat16)[None, None]
    grad_w_out = jnp.einsum("rtf,rtd->fd", activ_slots, upstream_slots, preferred_element_type=f32)
    grad_w_out = jnp.where(mine_out, grad_w_out, 0.0).astype(jnp.bfloat16)[None, None]
    return (layer_out, grad_tokens, grad_w_in, grad_w_out)


def solution(mesh):
    placed = (
        P("row", "col"),
        P("row", "col"),
        P("col", "row", None, None),
        P("col", None),
        P("col", "row", None, None),
        P("col", None),
    )
    return jax.shard_map(
        per_device,
        mesh=mesh,
        in_specs=placed,
        out_specs=(
            P("row", "col"),
            P("row", "col"),
            P("col", "row", None, None),
            P("col", "row", None, None),
        ),
        check_vma=False,
    )
```

time: 632 us -> 394 us (0.62)
  waiting for transfers between devices: 533 us -> 187 us
  blocking collectives: 0 us -> 91.4 us
  starting transfers between devices: 26.9 us -> 62.8 us
  between operations: 14.5 us -> 1.02 us
    all_gather x4 -> x0, waiting for transfers between devices: 297 us -> none  [the longest x1 88.4 us: per_device(): lax.all_gather(upstream, 'col', axis=1, tiled=True)]
    unnamed x8 -> x0, waiting for transfers between devices: 230 us -> none
    all_to_all x4 -> x8, waiting for transfers between devices: 6.18 us -> 187 us  [exchange(): return lax.all_to_all(blocks, axis, split_axis=0, concat_axis=0, tiled=True)]
    all_to_all x0 -> x2, blocking collectives: none -> 91.4 us  [exchange(): return lax.all_to_all(blocks, axis, split_axis=0, concat_axis=0, tiled=True)]
    all_to_all x4 -> x8, starting transfers between devices: 26.5 us -> 62.8 us  [exchange(): return lax.all_to_all(blocks, axis, split_axis=0, concat_axis=0, tiled=True)]
    unnamed x38 -> x20, local copies, waits for them, and re-layouts: 10.1 us -> 1.99 us
    dot_general x10 -> x8, matrix products: 22.3 us -> 19.8 us  [the longest x1 3.28 us: per_device(): jnp.einsum('rtd,rtn->dn', token_slots, grad_slots, preferred_element_type...]
  transfers between devices with their start and end apart: 10 -> 8, of which waited for: 7 -> 8; matrix products, arithmetic and copies ran while one was open for 7% -> 11% of each run, Pallas kernels for 0% -> 0%
where the time goes in v1:
time: 394 us; the launch traced here: 391 us
  waiting for transfers between devices  187 us (47%)
  blocking collectives  91.4 us (23%)
  starting transfers between devices  62.8 us (16%)
  local copies, waits for them, and re-layouts  20.9 us (5%)
  matrix products  19.8 us (5%)
  other arithmetic  7.58 us (2%)
    all_to_all x8, waiting for transfers between devices, exchange(): return lax.all_to_all(blocks, axis, split_axis=0, concat_axis=0, tiled=True)  187 us
    all_to_all x2, blocking collectives, exchange(): return lax.all_to_all(blocks, axis, split_axis=0, concat_axis=0, tiled=True)  91.4 us
    all_to_all x8, starting transfers between devices, exchange(): return lax.all_to_all(blocks, axis, split_axis=0, concat_axis=0, tiled=True)  62.8 us
  transfers between devices with their start and end apart: 8, of which 8 were waited for; matrix products, arithmetic and copies ran while one was open for 11% of the time, Pallas kernels for 0%

profile of v1, /device:TPU:1, one launch (start us, length us, event | category | flops | bytes accessed | tf_op | source)
XLA Modules:
  0.0 390.7 jit_solution(3871787656317129795)
XLA Ops:
  0.6 0.9 copy.31
  1.5 1.2 broadcast_in_dim.35
  2.8 11.2 %all-to-all-start = ((bf16[32,128,128]{1,2,0:T(8,128)(2,1)}), bf16[32,128,128]{1,2,0:T(8,128)(2,1)S(1)}, u32[]{:S(2)}, u32[]{:S(2)}) async-start(bf16[32,128,128]{1,2,0:T(8,128)(2,1)} %broadcast_in_dim.35), calls=%async_computation | async-start | bytes 2097152 | tf_op jit(solution)/shard_map/all_to_all | solution.py:27
  14.0 0.0 copy-start.4
  14.0 0.1 copy.39
  14.1 27.6 %all-to-all-done = bf16[32,128,128]{1,2,0:T(8,128)(2,1)S(1)} async-done(((bf16[32,128,128]{1,2,0:T(8,128)(2,1)}), bf16[32,128,128]{1,2,0:T(8,128)(2,1)S(1)}, u32[]{:S(2)}, u32[]{:S(2)}) %all-to-all-start) | async-done | bytes 1048608 | tf_op jit(solution)/shard_map/all_to_all | solution.py:27
  41.7 0.2 broadcast_in_dim.44
  42.0 33.9 %all_to_all.50 = bf16[32,128,128]{1,2,0:T(8,128)(2,1)} all-to-all(bf16[32,128,128]{1,2,0:T(8,128)(2,1)S(1)} %broadcast_in_dim.44), channel_id=1, replica_groups=mesh['row'=16,'col'=32] {'col'}, dimensions={0} | all-to-all | bytes 2097152 | tf_op jit(solution)/shard_map/all_to_all | solution.py:27
  75.8 0.0 copy-done.4
  75.8 0.2 broadcast_in_dim.40
  76.0 0.0 copy-start.5
  76.0 57.6 %all_to_all.51 = bf16[16,256,256]{2,1,0:T(8,128)(2,1)} all-to-all(bf16[16,256,256]{2,1,0:T(8,128)(2,1)S(1)} %broadcast_in_dim.40), channel_id=1, replica_groups=mesh['row'=16,'col'=32] {'row'}, dimensions={0} | all-to-all | bytes 4194304 | tf_op jit(solution)/shard_map/all_to_all | solution.py:27
  133.6 1.5 broadcast_in_dim.42
  135.1 4.4 %all-to-all-start.2 = ((bf16[16,256,256]{2,1,0:T(8,128)(2,1)}), bf16[16,256,256]{2,1,0:T(8,128)(2,1)S(1)}, u32[]{:S(2)}, u32[]{:S(2)}) async-start(bf16[16,256,256]{2,1,0:T(8,128)(2,1)} %broadcast_in_dim.42), calls=%async_computation.2 | async-start | bytes 4194304 | tf_op jit(solution)/shard_map/all_to_all | solution.py:27
  139.6 1.5 copy.32
  141.1 1.6 gather_fusion
  142.7 1.6 copy.33
  144.3 0.0 copy-start.8
  144.3 1.2 broadcast_select_fusion.3
  145.5 42.1 %all-to-all-done.2 = bf16[16,256,256]{2,1,0:T(8,128)(2,1)S(1)} async-done(((bf16[16,256,256]{2,1,0:T(8,128)(2,1)}), bf16[16,256,256]{2,1,0:T(8,128)(2,1)S(1)}, u32[]{:S(2)}, u32[]{:S(2)}) %all-to-all-start.2) | async-done | bytes 2097184 | tf_op jit(solution)/shard_map/all_to_all | solution.py:27
  187.6 5.3 %all-to-all-start.6 = ((bf16[16,128,256]{1,2,0:T(8,128)(2,1)}), bf16[16,128,256]{1,2,0:T(8,128)(2,1)}, u32[]{:S(2)}, u32[]{:S(2)}) async-start(bf16[16,128,256]{1,2,0:T(8,128)(2,1)} %broadcast_select_fusion.3), calls=%async_computation.6 | async-start | bytes 2097152 | tf_op jit(solution)/shard_map/all_to_all | solution.py:27
  193.0 0.1 fusion.20
  193.1 1.3 copy.40
  194.4 1.8 gather_fusion.2
  196.3 1.1 broadcast_select_fusion.1
  197.4 20.1 %all-to-all-done.6 = bf16[16,128,256]{1,2,0:T(8,128)(2,1)} async-done(((bf16[16,128,256]{1,2,0:T(8,128)(2,1)}), bf16[16,128,256]{1,2,0:T(8,128)(2,1)}, u32[]{:S(2)}, u32[]{:S(2)}) %all-to-all-start.6) | async-done | bytes 1048608 | tf_op jit(solution)/shard_map/all_to_all | solution.py:27
  217.5 7.2 %all-to-all-start.9 = ((bf16[16,128,256]{2,1,0:T(8,128)(2,1)}), bf16[16,128,256]{2,1,0:T(8,128)(2,1)}, u32[]{:S(2)}, u32[]{:S(2)}) async-start(bf16[16,128,256]{2,1,0:T(8,128)(2,1)} %broadcast_select_fusion.1), calls=%async_computation.9 | async-start | bytes 2097152 | tf_op jit(solution)/shard_map/all_to_all | solution.py:27
  224.7 0.1 fusion.25
  224.8 2.4 fusion.38
  227.2 0.4 multiply_reduce_fusion.1
  227.7 2.0 fusion.40
  229.7 0.4 multiply_reduce_fusion
  230.2 0.1 multiply_convert_fusion
  230.3 0.6 gather_fusion.3
  230.9 1.2 broadcast_select_fusion
  232.1 17.1 %all-to-all-done.9 = bf16[16,128,256]{2,1,0:T(8,128)(2,1)} async-done(((bf16[16,128,256]{2,1,0:T(8,128)(2,1)}), bf16[16,128,256]{2,1,0:T(8,128)(2,1)}, u32[]{:S(2)}, u32[]{:S(2)}) %all-to-all-start.9) | async-done | bytes 1048608 | tf_op jit(solution)/shard_map/all_to_all | solution.py:27
  249.2 7.3 %all-to-all-start.7 = ((bf16[16,128,256]{2,1,0:T(8,128)(2,1)}), bf16[16,128,256]{2,1,0:T(8,128)(2,1)}, u32[]{:S(2)}, u32[]{:S(2)}) async-start(bf16[16,128,256]{2,1,0:T(8,128)(2,1)} %broadcast_select_fusion), calls=%async_computation.7 | async-start | bytes 2097152 | tf_op jit(solution)/shard_map/all_to_all | solution.py:27
  256.5 1.6 gather_fusion.1
  258.1 1.6 copy.35
  259.7 1.1 broadcast_select_fusion.2
  260.8 20.1 %all-to-all-done.7 = bf16[16,128,256]{2,1,0:T(8,128)(2,1)} async-done(((bf16[16,128,256]{2,1,0:T(8,128)(2,1)}), bf16[16,128,256]{2,1,0:T(8,128)(2,1)}, u32[]{:S(2)}, u32[]{:S(2)}) %all-to-all-start.7) | async-done | bytes 1048608 | tf_op jit(solution)/shard_map/all_to_all | solution.py:27
  281.0 7.2 %all-to-all-start.8 = ((bf16[16,128,256]{1,2,0:T(8,128)(2,1)}), bf16[16,128,256]{1,2,0:T(8,128)(2,1)S(1)}, u32[]{:S(2)}, u32[]{:S(2)}) async-start(bf16[16,128,256]{1,2,0:T(8,128)(2,1)} %broadcast_select_fusion.2), calls=%async_computation.8 | async-start | bytes 2097152 | tf_op jit(solution)/shard_map/all_to_all | solution.py:27
  288.2 2.7 fusion.41
  290.9 2.3 fusion.7
  293.2 0.2 fusion.36
  293.4 0.1 pad_maximum_fusion.1
  293.5 1.3 copy.42
  294.8 18.5 %all-to-all-done.8 = bf16[16,128,256]{1,2,0:T(8,128)(2,1)S(1)} async-done(((bf16[16,128,256]{1,2,0:T(8,128)(2,1)}), bf16[16,128,256]{1,2,0:T(8,128)(2,1)S(1)}, u32[]{:S(2)}, u32[]{:S(2)}) %all-to-all-start.8) | async-done | bytes 1048608 | tf_op jit(solution)/shard_map/all_to_all | solution.py:27
  313.3 1.0 copy-done.2
  314.2 13.9 %all-to-all-start.5 = ((bf16[32,128,128]{2,1,0:T(8,128)(2,1)}), bf16[32,128,128]{2,1,0:T(8,128)(2,1)S(1)}, u32[]{:S(2)}, u32[]{:S(2)}) async-start(bf16[32,128,128]{2,1,0:T(8,128)(2,1)} %bitcast.86), calls=%async_computation.5 | async-start | bytes 2097152 | tf_op jit(solution)/shard_map/all_to_all | solution.py:27
  328.1 1.7 fusion.39
  329.9 2.3 fusion.4
  332.2 0.2 fusion.37
  332.4 0.1 pad_maximum_fusion
  332.5 1.3 copy.38
  333.7 22.1 %all-to-all-done.5 = bf16[32,128,128]{2,1,0:T(8,128)(2,1)S(1)} async-done(((bf16[32,128,128]{2,1,0:T(8,128)(2,1)}), bf16[32,128,128]{2,1,0:T(8,128)(2,1)S(1)}, u32[]{:S(2)}, u32[]{:S(2)}) %all-to-all-start.5) | async-done | bytes 1048608 | tf_op jit(solution)/shard_map/all_to_all | solution.py:27
  355.9 6.3 %all-to-all-start.3 = ((bf16[32,128,128]{2,1,0:T(8,128)(2,1)}), bf16[32,128,128]{2,1,0:T(8,128)(2,1)S(1)}, u32[]{:S(2)}, u32[]{:S(2)}) async-start(bf16[32,128,128]{2,1,0:T(8,128)(2,1)} %bitcast.14), calls=%async_computation.3 | async-start | bytes 2097152 | tf_op jit(solution)/shard_map/all_to_all | solution.py:27
  362.2 0.6 constant_dynamic-slice_fusion.1
  362.8 0.6 constant_dynamic-slice_fusion
  363.4 3.3 fusion.14
  366.7 3.0 fusion.15
  369.6 0.8 reduce_sum.45
  370.4 19.5 %all-to-all-done.3 = bf16[32,128,128]{2,1,0:T(8,128)(2,1)S(1)} async-done(((bf16[32,128,128]{2,1,0:T(8,128)(2,1)}), bf16[32,128,128]{2,1,0:T(8,128)(2,1)S(1)}, u32[]{:S(2)}, u32[]{:S(2)}) %all-to-all-start.3) | async-done | bytes 1048608 | tf_op jit(solution)/shard_map/all_to_all | solution.py:27
  390.0 0.8 reduce_sum.43
  (25 shorter events, 0.1 us)
Async XLA Ops:
  0.6 13.4 %copy-start.6 = (bf16[128,128]{1,0:T(8,128)(2,1)S(1)}, bf16[128,128]{1,0:T(8,128)(2,1)}, u32[]{:S(2)}) copy-start(bf16[128,128]{1,0:T(8,128)(2,1)} %param.11) | copy-start | bytes 98308
  2.8 39.0 %all-to-all-start = ((bf16[32,128,128]{1,2,0:T(8,128)(2,1)}), bf16[32,128,128]{1,2,0:T(8,128)(2,1)S(1)}, u32[]{:S(2)}, u32[]{:S(2)}) async-start(bf16[32,128,128]{1,2,0:T(8,128)(2,1)} %broadcast_in_dim.35), calls=%async_computation | async-start | bytes 2097152 | tf_op jit(solution)/shard_map/all_to_all | solution.py:27
  14.0 61.8 %copy-start.4 = (bf16[1,1,256,256]{3,2,1,0:T(8,128)(2,1)S(1)}, bf16[1,1,256,256]{3,2,1,0:T(8,128)(2,1)}, u32[]{:S(2)}) copy-start(bf16[1,1,256,256]{3,2,1,0:T(8,128)(2,1)} %param.12) | copy-start | bytes 393220
  41.7 34.3 %copy-start.1 = (bf16[32,128,128]{1,2,0:T(8,128)(2,1)}, bf16[32,128,128]{1,2,0:T(8,128)(2,1)S(1)}, u32[]{:S(2)}) copy-start(bf16[32,128,128]{1,2,0:T(8,128)(2,1)S(1)} %all-to-all-done) | copy-start | bytes 3145732
  76.0 57.6 %copy-start.5 = (bf16[1,1,256,256]{3,2,1,0:T(8,128)(2,1)S(1)}, bf16[1,1,256,256]{3,2,1,0:T(8,128)(2,1)}, u32[]{:S(2)}) copy-start(bf16[1,1,256,256]{3,2,1,0:T(8,128)(2,1)} %param.14) | copy-start | bytes 393220
  135.1 4.4 %copy-start.7 = (s32[1,16]{1,0:T(1,128)S(1)}, s32[1,16]{1,0:T(1,128)}, u32[]{:S(2)}) copy-start(s32[1,16]{1,0:T(1,128)} %param.13) | copy-start | bytes 196
  135.1 52.5 %all-to-all-start.2 = ((bf16[16,256,256]{2,1,0:T(8,128)(2,1)}), bf16[16,256,256]{2,1,0:T(8,128)(2,1)S(1)}, u32[]{:S(2)}, u32[]{:S(2)}) async-start(bf16[16,256,256]{2,1,0:T(8,128)(2,1)} %broadcast_in_dim.42), calls=%async_computation.2 | async-start | bytes 4194304 | tf_op jit(solution)/shard_map/all_to_all | solution.py:27
  144.3 48.6 %copy-start.8 = (s32[1,16]{1,0:T(1,128)S(1)}, s32[1,16]{1,0:T(1,128)}, u32[]{:S(2)}) copy-start(s32[1,16]{1,0:T(1,128)} %param.15) | copy-start | bytes 196
  145.5 47.6 %copy-start = (bf16[32,128,128]{1,2,0:T(8,128)(2,1)S(1)}, bf16[32,128,128]{1,2,0:T(8,128)(2,1)}, u32[]{:S(2)}) copy-start(bf16[32,128,128]{1,2,0:T(8,128)(2,1)} %all_to_all.50) | copy-start | bytes 3145732
  187.6 29.8 %all-to-all-start.6 = ((bf16[16,128,256]{1,2,0:T(8,128)(2,1)}), bf16[16,128,256]{1,2,0:T(8,128)(2,1)}, u32[]{:S(2)}, u32[]{:S(2)}) async-start(bf16[16,128,256]{1,2,0:T(8,128)(2,1)} %broadcast_select_fusion.3), calls=%async_computation.6 | async-start | bytes 2097152 | tf_op jit(solution)/shard_map/all_to_all | solution.py:27
  217.5 31.7 %all-to-all-start.9 = ((bf16[16,128,256]{2,1,0:T(8,128)(2,1)}), bf16[16,128,256]{2,1,0:T(8,128)(2,1)}, u32[]{:S(2)}, u32[]{:S(2)}) async-start(bf16[16,128,256]{2,1,0:T(8,128)(2,1)} %broadcast_select_fusion.1), calls=%async_computation.9 | async-start | bytes 2097152 | tf_op jit(solution)/shard_map/all_to_all | solution.py:27
  249.2 31.8 %all-to-all-start.7 = ((bf16[16,128,256]{2,1,0:T(8,128)(2,1)}), bf16[16,128,256]{2,1,0:T(8,128)(2,1)}, u32[]{:S(2)}, u32[]{:S(2)}) async-start(bf16[16,128,256]{2,1,0:T(8,128)(2,1)} %broadcast_select_fusion), calls=%async_computation.7 | async-start | bytes 2097152 | tf_op jit(solution)/shard_map/all_to_all | solution.py:27
  281.0 32.3 %all-to-all-start.8 = ((bf16[16,128,256]{1,2,0:T(8,128)(2,1)}), bf16[16,128,256]{1,2,0:T(8,128)(2,1)S(1)}, u32[]{:S(2)}, u32[]{:S(2)}) async-start(bf16[16,128,256]{1,2,0:T(8,128)(2,1)} %broadcast_select_fusion.2), calls=%async_computation.8 | async-start | bytes 2097152 | tf_op jit(solution)/shard_map/all_to_all | solution.py:27
  313.3 1.0 copy-start.2
  314.2 41.6 %all-to-all-start.5 = ((bf16[32,128,128]{2,1,0:T(8,128)(2,1)}), bf16[32,128,128]{2,1,0:T(8,128)(2,1)S(1)}, u32[]{:S(2)}, u32[]{:S(2)}) async-start(bf16[32,128,128]{2,1,0:T(8,128)(2,1)} %bitcast.86), calls=%async_computation.5 | async-start | bytes 2097152 | tf_op jit(solution)/shard_map/all_to_all | solution.py:27
  355.9 10.8 %copy-start.3 = (bf16[16,128,256]{1,2,0:T(8,128)(2,1)S(1)}, bf16[16,128,256]{1,2,0:T(8,128)(2,1)}, u32[]{:S(2)}) copy-start(bf16[16,128,256]{1,2,0:T(8,128)(2,1)} %copy-done.2) | copy-start | bytes 3145732
  355.9 34.1 %all-to-all-start.3 = ((bf16[32,128,128]{2,1,0:T(8,128)(2,1)}), bf16[32,128,128]{2,1,0:T(8,128)(2,1)S(1)}, u32[]{:S(2)}, u32[]{:S(2)}) async-start(bf16[32,128,128]{2,1,0:T(8,128)(2,1)} %bitcast.14), calls=%async_computation.3 | async-start | bytes 2097152 | tf_op jit(solution)/shard_map/all_to_all | solution.py:27

commit v2 on v1

v2 whole, which is shorter than its diff:
```python
import jax
import jax.numpy as jnp
from jax import lax
from jax.experimental import pallas as pl
from jax.experimental.pallas import tpu as pltpu
from jax.sharding import PartitionSpec as P

RING = 8
BF, F32 = jnp.bfloat16, jnp.float32


class Place:
    def __init__(self):
        row, col = lax.axis_index("row"), lax.axis_index("col")
        self.row, self.col = row, col
        self.z, self.lo = row // 2, row % 2
        self.hi, self.y, self.core = col // (2 * RING), (col // 2) % RING, col % 2

    def row_at(self, dz=0, lo=None):
        return lax.rem(self.z + dz + RING, RING) * 2 + (self.lo if lo is None else lo)

    def col_at(self, dy=0, hi=None, core=None):
        y = lax.rem(self.y + dy + RING, RING)
        hi = self.hi if hi is None else hi
        return (hi * RING + y) * 2 + (self.core if core is None else core)

    def peers(self):
        return {
            "z+": (self.row_at(1), self.col),
            "z-": (self.row_at(-1), self.col),
            "lo": (self.row_at(0, 1 - self.lo), self.col),
            "y+": (self.row, self.col_at(1)),
            "y-": (self.row, self.col_at(-1)),
            "hi": (self.row, self.col_at(0, 1 - self.hi)),
            "core": (self.row, self.col_at(0, None, 1 - self.core)),
        }


def meet(peers):
    barrier = pltpu.get_barrier_semaphore()
    for device in peers.values():
        pl.semaphore_signal(barrier, inc=1, device_id=device, device_id_type=pl.DeviceIdType.MESH)
    pl.semaphore_wait(barrier, len(peers))


class Sender:
    def __init__(self, sems, peers):
        self.sems, self.peers, self.started = sems, peers, []

    def copy(self, src, dst, recv_sem, peer):
        copy = pltpu.make_async_remote_copy(
            src_ref=src,
            dst_ref=dst,
            send_sem=self.sems.at[len(self.started)],
            recv_sem=recv_sem,
            device_id=self.peers[peer],
            device_id_type=pl.DeviceIdType.MESH,
        )
        copy.start()
        self.started.append(copy)

    def arrived(self, dst, recv_sem):
        pltpu.make_async_remote_copy(
            src_ref=dst,
            dst_ref=dst,
            send_sem=self.sems.at[0],
            recv_sem=recv_sem,
            device_id=self.peers["core"],
            device_id_type=pl.DeviceIdType.MESH,
        ).wait_recv()

    def drain(self):
        for copy in self.started:
            copy.wait_send()


GATHER_SENDS = 64


def gather_kernel(x_ref, wi_ref, wo_ref, xg, wig, wog, send_sems, x_sems, wi_sems, wo_sems, own_sems):
    at = Place()
    peers = at.peers()
    meet(peers)
    out = Sender(send_sems, peers)
    own = [
        pltpu.make_async_copy(x_ref, xg.at[at.col], own_sems.at[0]),
        pltpu.make_async_copy(wi_ref, wig.at[at.row], own_sems.at[1]),
        pltpu.make_async_copy(wo_ref, wog.at[at.row], own_sems.at[2]),
    ]

    def x_send(src, col, *to):
        for peer in to:
            out.copy(src, xg.at[col], x_sems.at[col], peer)

    def wi_send(src, row, *to):
        for peer in to:
            out.copy(src, wig.at[row], wi_sems.at[row], peer)

    def wo_send(src, row, *to):
        for peer in to:
            out.copy(src, wog.at[row], wo_sems.at[row], peer)

    x_send(x_ref, at.col, "hi", "y+", "y-", "core")
    wi_send(wi_ref, at.row, "lo", "z+", "z-")
    wo_send(wo_ref, at.row, "z+", "z-", "lo")
    for copy in own:
        copy.start()

    def x_pass(col, *to):
        out.arrived(xg.at[col], x_sems.at[col])
        x_send(xg.at[col], col, *to)

    def wi_pass(row, *to):
        out.arrived(wig.at[row], wi_sems.at[row])
        wi_send(wig.at[row], row, *to)

    def wo_pass(row, *to):
        out.arrived(wog.at[row], wo_sems.at[row])
        wo_send(wog.at[row], row, *to)

    x_pass(at.col_at(0, 1 - at.hi), "y+", "y-", "core")
    wi_pass(at.row_at(0, 1 - at.lo), "z+", "z-")
    half = RING // 2
    for step in range(1, half + 1):
        for sign, mark in ((-1, "+"), (1, "-")):
            if sign == 1 and step == half:
                continue
            last = step == half if sign == -1 else step == half - 1
            for hi in (at.hi, 1 - at.hi):
                x_pass(at.col_at(sign * step, hi), *(() if last else ("y" + mark,)), "core")
        for sign, mark in ((-1, "+"), (1, "-")):
            if sign == 1 and step == half:
                continue
            last = step == half if sign == -1 else step == half - 1
            onward = () if last else ("z" + mark,)
            wi_pass(at.row_at(sign * step), *onward)
            wo_pass(at.row_at(sign * step), *onward, "lo")
            wi_pass(at.row_at(sign * step, 1 - at.lo), *onward)
    for step in range(RING):
        for hi in range(2):
            col = at.col_at(step, hi, 1 - at.core)
            out.arrived(xg.at[col], x_sems.at[col])
        row = at.row_at(step, 1 - at.lo)
        out.arrived(wog.at[row], wo_sems.at[row])
    out.drain()
    for copy in own:
        copy.wait()


def gather(x, wi, wo):
    any_space = pl.BlockSpec(memory_space=pl.ANY)
    tile = wi.shape
    return pl.pallas_call(
        gather_kernel,
        name="gather_all",
        out_shape=(
            jax.ShapeDtypeStruct((4 * RING, *x.shape), BF),
            jax.ShapeDtypeStruct((2 * RING, *tile), BF),
            jax.ShapeDtypeStruct((2 * RING, *tile), BF),
        ),
        in_specs=[any_space] * 3,
        out_specs=(any_space,) * 3,
        scratch_shapes=[
            pltpu.SemaphoreType.DMA((GATHER_SENDS,)),
            pltpu.SemaphoreType.DMA((4 * RING,)),
            pltpu.SemaphoreType.DMA((2 * RING,)),
            pltpu.SemaphoreType.DMA((2 * RING,)),
            pltpu.SemaphoreType.DMA((3,)),
        ],
        compiler_params=pltpu.CompilerParams(collective_id=0, has_side_effects=True),
    )(x, wi, wo)


def dot(a, b, contract):
    return lax.dot_general(a, b, (contract, ((), ())), preferred_element_type=F32)


def panel_kernel(in_codes, out_codes, x, wi, wo, parts, grads, hid, gact, act, gh, lay, inp):
    slots = wi.shape[0]
    hid[...] = jnp.zeros_like(hid)
    gact[...] = jnp.zeros_like(gact)
    lay[...] = jnp.zeros_like(lay)
    inp[...] = jnp.zeros_like(inp)

    def codes(ref, k):
        code = ref[k]
        clipped = jnp.maximum(code, 0)
        return clipped // 2, clipped % 2, code >= 0

    def tile(which, i):
        return jnp.concatenate([x[2 * i, which], x[2 * i + 1, which]], axis=1)

    def inward(k, _):
        i, j, filled = codes(in_codes, k)

        @pl.when(filled)
        def _():
            hid[j] += dot(tile(0, i), wi[k], ((1,), (0,)))

        i2, j2, filled2 = codes(out_codes, k)

        @pl.when(filled2)
        def _():
            gact[j2] += dot(tile(1, i2), wo[k], ((1,), (1,)))

        return 0

    lax.fori_loop(0, slots, inward, 0)
    for j in range(2):
        h = hid[j]
        s = jax.nn.sigmoid(h)
        act[j] = (h * s).astype(BF)
        gh[j] = (gact[j] * (s * (1.0 + h * (1.0 - s)))).astype(BF)

    def outward(k, _):
        i, j, filled = codes(in_codes, k)

        @pl.when(filled)
        def _():
            g = gh[j]
            inp[i] += dot(g, wi[k], ((1,), (1,)))
            grads[0, k] = dot(tile(0, i), g, ((0,), (0,))).astype(BF)

        @pl.when(jnp.logical_not(filled))
        def _():
            grads[0, k] = jnp.zeros(grads.shape[2:], BF)

        i2, j2, filled2 = codes(out_codes, k)

        @pl.when(filled2)
        def _():
            a = act[j2]
            lay[i2] += dot(a, wo[k], ((1,), (0,)))
            grads[1, k] = dot(a, tile(1, i2), ((0,), (0,))).astype(BF)

        @pl.when(jnp.logical_not(filled2))
        def _():
            grads[1, k] = jnp.zeros(grads.shape[2:], BF)

        return 0

    lax.fori_loop(0, slots, outward, 0)

    def round_up(i, _):
        for t, total in enumerate((lay, inp)):
            full = total[i].astype(BF)
            for core in range(2):
                parts[core, i, t] = full[:, core * 128 : (core + 1) * 128]
        return 0

    lax.fori_loop(0, lay.shape[0], round_up, 0)


def panel(in_codes, out_codes, x, wi, wo):
    cols, _, rows, width = x.shape
    tiles = cols // 2
    slots, size, _ = wi.shape
    vmem, smem = pl.BlockSpec(memory_space=pltpu.VMEM), pl.BlockSpec(memory_space=pltpu.SMEM)
    return pl.pallas_call(
        panel_kernel,
        name="panel",
        out_shape=(
            jax.ShapeDtypeStruct((2, tiles, 2, rows, width), BF),
            jax.ShapeDtypeStruct((2, slots, size, size), BF),
        ),
        in_specs=[smem, smem, vmem, vmem, vmem],
        out_specs=(vmem, vmem),
        scratch_shapes=[
            pltpu.VMEM((2, rows, size), F32),
            pltpu.VMEM((2, rows, size), F32),
            pltpu.VMEM((2, rows, size), BF),
            pltpu.VMEM((2, rows, size), BF),
            pltpu.VMEM((tiles, rows, size), F32),
            pltpu.VMEM((tiles, rows, size), F32),
        ],
        compiler_params=pltpu.CompilerParams(vmem_limit_bytes=48 << 20),
    )(in_codes, out_codes, x, wi, wo)


REDUCE_SENDS = 48


def reduce_kernel(
    parts, grads, red, grad_out,
    pair_buf, chip_sum, y_buf, z_buf, hi_buf, lo_buf, hi_sum, lo_sum,
    send_sems, pair_sem, y_sems, z_sems, hi_sem, lo_sem,
):
    at = Place()
    peers = at.peers()
    meet(peers)
    out = Sender(send_sems, peers)
    half = RING // 2
    far = (half, half - 1)
    marks = ("+", "-")
    signs = (1, -1)

    def wide(value):
        return value.astype(F32)

    def z_of(sign, dist):
        return lax.rem(at.z + sign * dist + RING, RING)

    def y_of(sign, dist):
        return lax.rem(at.y + sign * dist + RING, RING)

    out.copy(parts.at[1 - at.core], pair_buf, pair_sem, "core")
    for d in range(2):
        for lo in range(2):
            for t in range(2):
                slot = d * half
                out.copy(
                    grads.at[t, z_of(signs[d], far[d]) * 2 + lo],
                    z_buf.at[slot, lo, t],
                    z_sems.at[slot, lo, t],
                    "z" + marks[d],
                )
    out.arrived(pair_buf, pair_sem)
    for hi in range(2):
        for y in range(RING):
            i = hi * RING + y
            chip_sum[y, hi] = (wide(parts[at.core, i]) + wide(pair_buf[i])).astype(BF)
    for d in range(2):
        slot = d * half
        out.copy(chip_sum.at[y_of(signs[d], far[d])], y_buf.at[slot], y_sems.at[slot], "y" + marks[d])

    for step in range(1, half):
        for d in range(2):
            if step >= far[d]:
                continue
            slot = d * half + step - 1
            out.arrived(y_buf.at[slot], y_sems.at[slot])
            target = y_of(signs[d], far[d] - step)
            y_buf[slot] = (wide(y_buf[slot]) + wide(chip_sum[target])).astype(BF)
            out.copy(y_buf.at[slot], y_buf.at[slot + 1], y_sems.at[slot + 1], "y" + marks[d])
        for lo in range(2):
            for t in range(2):
                for d in range(2):
                    if step >= far[d]:
                        continue
                    slot = d * half + step - 1
                    out.arrived(z_buf.at[slot, lo, t], z_sems.at[slot, lo, t])
                    target = z_of(signs[d], far[d] - step) * 2 + lo
                    z_buf[slot, lo, t] = (wide(z_buf[slot, lo, t]) + wide(grads[t, target])).astype(BF)
                    out.copy(
                        z_buf.at[slot, lo, t],
                        z_buf.at[slot + 1, lo, t],
                        z_sems.at[slot + 1, lo, t],
                        "z" + marks[d],
                    )

    ends = [d * half + far[d] - 1 for d in range(2)]
    for slot in ends:
        out.arrived(y_buf.at[slot], y_sems.at[slot])

    def y_total(hi):
        return wide(chip_sum[at.y, hi]) + wide(y_buf[ends[0], hi]) + wide(y_buf[ends[1], hi])

    hi_sum[...] = y_total(1 - at.hi).astype(BF)
    out.copy(hi_sum, hi_buf, hi_sem, "hi")

    def z_total(lo, t):
        return wide(grads[t, at.z * 2 + lo]) + wide(z_buf[ends[0], lo, t]) + wide(z_buf[ends[1], lo, t])

    for t in range(2):
        for lo in range(2):
            for slot in ends:
                out.arrived(z_buf.at[slot, lo, t], z_sems.at[slot, lo, t])
        lo_sum[t] = z_total(1 - at.lo, t).astype(BF)
        out.copy(lo_sum.at[t], lo_buf.at[t], lo_sem.at[t], "lo")
    out.arrived(hi_buf, hi_sem)
    red[...] = (y_total(at.hi) + wide(hi_buf[...])).astype(BF)
    for t in range(2):
        out.arrived(lo_buf.at[t], lo_sem.at[t])
        grad_out[t] = (z_total(at.lo, t) + wide(lo_buf[t])).astype(BF)
    out.drain()


def reduce(parts, grads):
    _, tiles, two, rows, width = parts.shape
    size = grads.shape[-1]
    vmem = pl.BlockSpec(memory_space=pltpu.VMEM)
    block, tile = (two, rows, width), (size, size)
    return pl.pallas_call(
        reduce_kernel,
        name="reduce_all",
        out_shape=(jax.ShapeDtypeStruct(block, BF), jax.ShapeDtypeStruct((2, *tile), BF)),
        in_specs=[vmem, vmem],
        out_specs=(vmem, vmem),
        scratch_shapes=[
            pltpu.VMEM((tiles, *block), BF),
            pltpu.VMEM((RING, 2, *block), BF),
            pltpu.VMEM((RING - 1, 2, *block), BF),
            pltpu.VMEM((RING - 1, 2, 2, *tile), BF),
            pltpu.VMEM(block, BF),
            pltpu.VMEM((2, *tile), BF),
            pltpu.VMEM(block, BF),
            pltpu.VMEM((2, *tile), BF),
            pltpu.SemaphoreType.DMA((REDUCE_SENDS,)),
            pltpu.SemaphoreType.DMA,
            pltpu.SemaphoreType.DMA((RING - 1,)),
            pltpu.SemaphoreType.DMA((RING - 1, 2, 2)),
            pltpu.SemaphoreType.DMA,
            pltpu.SemaphoreType.DMA((2,)),
        ],
        compiler_params=pltpu.CompilerParams(
            collective_id=1, has_side_effects=True, vmem_limit_bytes=48 << 20
        ),
    )(parts, grads)


def per_device(tokens, upstream, w_in, in_codes, w_out, out_codes):
    x, wi, wo = gather(jnp.stack([tokens, upstream]), w_in[0, 0], w_out[0, 0])
    parts, grads = panel(in_codes[0], out_codes[0], x, wi, wo)
    red, grad = reduce(parts, grads)
    return red[0], red[1], grad[0][None, None], grad[1][None, None]


def solution(mesh):
    placed = (
        P("row", "col"),
        P("row", "col"),
        P("col", "row", None, None),
        P("col", None),
        P("col", "row", None, None),
        P("col", None),
    )
    return jax.shard_map(
        per_device,
        mesh=mesh,
        in_specs=placed,
        out_specs=(
            P("row", "col"),
            P("row", "col"),
            P("col", "row", None, None),
            P("col", "row", None, None),
        ),
        check_vma=False,
    )
```

time: 394 us -> 131 us (0.33)
  waiting for transfers between devices: 187 us -> 0 us
  Pallas kernels: 0 us -> 125 us
  blocking collectives: 91.4 us -> 0 us
  starting transfers between devices: 62.8 us -> 0 us
  matrix products: 19.8 us -> 0 us
  local copies, waits for them, and re-layouts: 20.9 us -> 4.24 us
  other arithmetic: 7.58 us -> 1.41 us
    all_to_all x8 -> x0, waiting for transfers between devices: 187 us -> none  [exchange(): return lax.all_to_all(blocks, axis, split_axis=0, concat_axis=0, tiled=True)]
    pallas_call x0 -> x3, Pallas kernels: none -> 125 us  [the longest x1 59.4 us: reduce(): pl.pallas_call(reduce_kernel, name='reduce_all', out_shape=(jax.ShapeDtyp...]
    all_to_all x2 -> x0, blocking collectives: 91.4 us -> none  [exchange(): return lax.all_to_all(blocks, axis, split_axis=0, concat_axis=0, tiled=True)]
    all_to_all x8 -> x0, starting transfers between devices: 62.8 us -> none  [exchange(): return lax.all_to_all(blocks, axis, split_axis=0, concat_axis=0, tiled=True)]
    dot_general x8 -> x0, matrix products: 19.8 us -> none  [the longest x1 3.28 us: per_device(): jnp.einsum('rtd,rtn->dn', token_slots, grad_slots, preferred_element_type...]
    gather x6 -> x0, local copies, waits for them, and re-layouts: 8.88 us -> none  [the longest x2 3.23 us: per_device(): picked_tokens = jnp.take(token_tiles, in_row, axis=0)]
    select_n x8 -> x0, other arithmetic: 4.64 us -> none  [the longest x2 1.17 us: per_device(): picked_tokens = jnp.take(token_tiles, in_row, axis=0)]
  transfers between devices with their start and end apart: 8 -> 0, of which waited for: 8 -> 0; matrix products, arithmetic and copies ran while one was open for 11% -> 0% of each run, Pallas kernels for 0% -> 0%
where the time goes in v2:
time: 131 us
  Pallas kernels  125 us (95%)
  local copies, waits for them, and re-layouts  4.24 us (3%)
  other arithmetic  1.41 us (1%)
    pallas_call x1, Pallas kernels, reduce(): pl.pallas_call(reduce_kernel, name='reduce_all', out_shape=(jax.ShapeDtyp...  59.4 us
    pallas_call x1, Pallas kernels, gather(): pl.pallas_call(gather_kernel, name='gather_all', out_shape=(jax.ShapeDtyp...  50.1 us
    pallas_call x1, Pallas kernels, panel(): pl.pallas_call(panel_kernel, name='panel', out_shape=(jax.ShapeDtypeStruc...  15.1 us
    unnamed x6, local copies, waits for them, and re-layouts  2.89 us

profile of v2, /device:TPU:1, one launch (start us, length us, event | category | flops | bytes accessed | tf_op | source)
XLA Modules:
  0.0 130.9 jit_solution(462162944192892493)
XLA Ops:
  0.6 1.4 %pad_maximum_fusion.x_ref = bf16[2,128,128]{2,1,0:T(8,128)(2,1)} fusion(bf16[1,128,128]{2,1,0:T(8,128)(2,1)} %bitcast.18, bf16[1,128,128]{2,1,0:T(8,128)(2,1)} %bitcast.19), kind=kLoop, calls=%fused_computation.2 | loop fusion | flops 32768 | bytes 131072 | tf_op jit(solution)/shard_map/stack | solution.py:412
  2.0 50.1 %gather_all.1 = (bf16[32,2,128,128]{3,2,1,0:T(8,128)(2,1)}, bf16[16,256,256]{2,1,0:T(8,128)(2,1)}, bf16[16,256,256]{2,1,0:T(8,128)(2,1)}) custom-call(bf16[2,128,128]{2,1,0:T(8,128)(2,1)} %pad_maximum_fusion.x_ref, bf16[256,256]{1,0:T(8,128)(2,1)} %bitcast.16, bf16[256,256]{1,0:T(8,128)(2,1)} %bitcast.17), custom_call_target="tpu_custom_call" | custom-call | tf_op jit(solution)/shard_map/gather_all/pallas_call | solution.py:153
  52.2 0.0 copy-start
  52.2 1.6 %copy-done = bf16[32,2,128,128]{3,2,1,0:T(8,128)(2,1)S(1)} copy-done((bf16[32,2,128,128]{3,2,1,0:T(8,128)(2,1)S(1)}, bf16[32,2,128,128]{3,2,1,0:T(8,128)(2,1)}, u32[]{:S(2)}) %copy-start) | copy-done | bytes 2097176
  53.8 0.0 copy-start.1
  53.8 0.7 copy-done.1
  54.4 0.0 copy-start.2
  54.4 0.7 copy-done.2
  55.1 15.1 %panel.1 = (bf16[2,16,2,128,128]{4,3,2,1,0:T(8,128)(2,1)S(1)}, bf16[2,16,256,256]{3,2,1,0:T(8,128)(2,1)}) custom-call(s32[16]{0:T(128)S(1)} %bitcast.14, s32[16]{0:T(128)S(1)} %bitcast.15, bf16[32,2,128,128]{3,2,1,0:T(8,128)(2,1)S(1)} %copy-done, bf16[16,256,256]{2,1,0:T(8,128)(2,1)} %get-tuple-element.12.wi, bf16[16,256,256]{2,1,0:T(8,128)(2,1)} %get-tuple-element.13.wo), custom_call_target="tpu_custom_call" | custom-call | tf_op jit(solution)/shard_map/panel/pallas_call | solution.py:259
  70.2 59.4 %reduce_all.1 = (bf16[2,128,128]{2,1,0:T(8,128)(2,1)S(1)}, bf16[2,256,256]{2,1,0:T(8,128)(2,1)S(1)}) custom-call(bf16[2,16,2,128,128]{4,3,2,1,0:T(8,128)(2,1)S(1)} %get-tuple-element.14.parts, bf16[2,16,256,256]{3,2,1,0:T(8,128)(2,1)} %get-tuple-element.15.grads), custom_call_target="tpu_custom_call" | custom-call | tf_op jit(solution)/shard_map/reduce_all/pallas_call | solution.py:383
  129.6 0.6 slice_bitcast_fusion.2
  130.2 0.7 slice_bitcast_fusion
Async XLA Ops:
  52.2 1.6 %copy-start = (bf16[32,2,128,128]{3,2,1,0:T(8,128)(2,1)S(1)}, bf16[32,2,128,128]{3,2,1,0:T(8,128)(2,1)}, u32[]{:S(2)}) copy-start(bf16[32,2,128,128]{3,2,1,0:T(8,128)(2,1)} %get-tuple-element.11.x) | copy-start | bytes 6291460
  53.8 0.7 copy-start.1
  54.4 0.7 copy-start.2

commit v3 on v1

v3 whole, which is shorter than its diff:
```python
import jax
import jax.numpy as jnp
from jax import lax
from jax.experimental import pallas as pl
from jax.experimental.pallas import tpu as pltpu
from jax.sharding import PartitionSpec as P

RING = 8
BF, F32 = jnp.bfloat16, jnp.float32


class Place:
    def __init__(self):
        row, col = lax.axis_index("row"), lax.axis_index("col")
        self.row, self.col = row, col
        self.z, self.lo = row // 2, row % 2
        self.hi, self.y, self.core = col // (2 * RING), (col // 2) % RING, col % 2

    def row_at(self, dz=0, lo=None):
        return lax.rem(self.z + dz + RING, RING) * 2 + (self.lo if lo is None else lo)

    def col_at(self, dy=0, hi=None, core=None):
        y = lax.rem(self.y + dy + RING, RING)
        hi = self.hi if hi is None else hi
        return (hi * RING + y) * 2 + (self.core if core is None else core)

    def peers(self):
        return {
            "z+": (self.row_at(1), self.col),
            "z-": (self.row_at(-1), self.col),
            "lo": (self.row_at(0, 1 - self.lo), self.col),
            "y+": (self.row, self.col_at(1)),
            "y-": (self.row, self.col_at(-1)),
            "hi": (self.row, self.col_at(0, 1 - self.hi)),
            "core": (self.row, self.col_at(0, None, 1 - self.core)),
        }


def meet(peers):
    barrier = pltpu.get_barrier_semaphore()
    for device in peers.values():
        pl.semaphore_signal(barrier, inc=1, device_id=device, device_id_type=pl.DeviceIdType.MESH)
    pl.semaphore_wait(barrier, len(peers))


class Sender:
    def __init__(self, sems, peers):
        self.sems, self.peers, self.started = sems, peers, []

    def copy(self, src, dst, recv_sem, peer):
        copy = pltpu.make_async_remote_copy(
            src_ref=src,
            dst_ref=dst,
            send_sem=self.sems.at[len(self.started)],
            recv_sem=recv_sem,
            device_id=self.peers[peer],
            device_id_type=pl.DeviceIdType.MESH,
        )
        copy.start()
        self.started.append(copy)

    def arrived(self, dst, recv_sem):
        pltpu.make_async_remote_copy(
            src_ref=dst,
            dst_ref=dst,
            send_sem=self.sems.at[0],
            recv_sem=recv_sem,
            device_id=self.peers["core"],
            device_id_type=pl.DeviceIdType.MESH,
        ).wait_recv()

    def drain(self):
        for copy in self.started:
            copy.wait_send()


GATHER_SENDS = 96


def dot(a, b, contract):
    return lax.dot_general(a, b, (contract, ((), ())), preferred_element_type=F32)


def split_code(ref, k):
    code = ref[k]
    clipped = jnp.maximum(code, 0)
    return clipped // 2, clipped % 2, code >= 0


def token_tile(x, which, i):
    halves = [jnp.concatenate([x[lo, 2 * i, which], x[lo, 2 * i + 1, which]], axis=1) for lo in range(2)]
    return jnp.concatenate(halves, axis=0)


def gather_kernel(
    in_codes, out_codes, tokens, upstream, wi_ref, wo_ref, xg, wig, wog, act, gh,
    hid, gact, mine, theirs, send_sems, x_sems, w_sems, own_sems, swap_sems,
):
    at = Place()
    peers = at.peers()
    x_own = xg.at[at.lo, at.col]
    own = [
        pltpu.make_async_copy(tokens, x_own.at[0], own_sems.at[0]),
        pltpu.make_async_copy(upstream, x_own.at[1], own_sems.at[1]),
        pltpu.make_async_copy(wi_ref, wig.at[at.z], own_sems.at[2]),
        pltpu.make_async_copy(wo_ref, wog.at[at.z], own_sems.at[3]),
    ]
    for copy in own:
        copy.start()
    meet(peers)
    out = Sender(send_sems, peers)
    for copy in own:
        copy.wait()
    held = (wig, wog)

    def x_send(lo, col, *to):
        for peer in to:
            out.copy(xg.at[lo, col], xg.at[lo, col], x_sems.at[lo, col], peer)

    def x_pass(lo, col, *to):
        out.arrived(xg.at[lo, col], x_sems.at[lo, col])
        x_send(lo, col, *to)

    def w_send(t, z, *to):
        for peer in to:
            out.copy(held[t].at[z], held[t].at[z], w_sems.at[t, z], peer)

    def w_pass(t, z, *to):
        out.arrived(held[t].at[z], w_sems.at[t, z])
        w_send(t, z, *to)

    x_send(at.lo, at.col, "lo", "hi", "y+", "y-")
    for t in range(2):
        w_send(t, at.z, "z+", "z-")
    x_send(at.lo, at.col, "core")
    x_pass(1 - at.lo, at.col, "hi", "y+", "y-", "core")
    x_pass(at.lo, at.col_at(0, 1 - at.hi), "y+", "y-", "core")
    x_pass(1 - at.lo, at.col_at(0, 1 - at.hi), "y+", "y-", "core")
    half = RING // 2
    flows = ((-1, "+"), (1, "-"))
    for step in range(1, half + 1):
        for d, (sign, mark) in enumerate(flows):
            for n, (lo, hi) in enumerate(((at.lo, at.hi), (1 - at.lo, at.hi), (at.lo, 1 - at.hi), (1 - at.lo, 1 - at.hi))):
                if step == half and n % 2 != d:
                    continue
                onward = step < half - 1 or (step == half - 1 and n % 2 == d)
                x_pass(lo, at.col_at(sign * step, hi), *(("y" + mark,) if onward else ()), "core")
        for t in range(2):
            for d, (sign, mark) in enumerate(flows):
                if step == half and t != d:
                    continue
                onward = step < half - 1 or (step == half - 1 and t == d)
                w_pass(t, lax.rem(at.z + sign * step + RING, RING), *(("z" + mark,) if onward else ()))
    for step in range(RING):
        for hi in range(2):
            for lo in range(2):
                col = at.col_at(step, hi, 1 - at.core)
                out.arrived(xg.at[lo, col], x_sems.at[lo, col])

    hid[...] = jnp.zeros_like(hid)
    gact[...] = jnp.zeros_like(gact)

    def inward(codes, which, weights, total, contract):
        def one(k, _):
            i, j, filled = split_code(codes, k)
            product = dot(token_tile(xg, which, i), weights[k], contract)
            for col in range(2):
                total[col] += jnp.where(jnp.logical_and(filled, j == col), product, 0.0)
            return 0

        lax.fori_loop(0, RING, one, 0)
        mine[which] = total[...].astype(BF)
        out.copy(mine.at[which], theirs.at[which], swap_sems.at[which], "lo")

    inward(in_codes, 0, wig, hid, ((1,), (0,)))
    inward(out_codes, 1, wog, gact, ((1,), (1,)))
    out.arrived(theirs.at[0], swap_sems.at[0])
    out.arrived(theirs.at[1], swap_sems.at[1])
    for j in range(2):
        h = hid[j] + theirs[0, j].astype(F32)
        s = jax.nn.sigmoid(h)
        act[j] = (h * s).astype(BF)
        gh[j] = ((gact[j] + theirs[1, j].astype(F32)) * (s * (1.0 + h * (1.0 - s)))).astype(BF)
    out.drain()


def specs():
    return pl.BlockSpec(memory_space=pltpu.VMEM), pl.BlockSpec(memory_space=pltpu.SMEM)


def gather(in_codes, out_codes, tokens, upstream, wi, wo):
    vmem, smem = specs()
    size = wi.shape[0]
    pair = (2, 2 * tokens.shape[0], size)
    return pl.pallas_call(
        gather_kernel,
        name="gather_all",
        out_shape=(
            jax.ShapeDtypeStruct((2, 4 * RING, 2, *tokens.shape), BF),
            jax.ShapeDtypeStruct((RING, *wi.shape), BF),
            jax.ShapeDtypeStruct((RING, *wi.shape), BF),
            jax.ShapeDtypeStruct(pair, BF),
            jax.ShapeDtypeStruct(pair, BF),
        ),
        in_specs=[smem, smem, vmem, vmem, vmem, vmem],
        out_specs=(vmem,) * 5,
        scratch_shapes=[
            pltpu.VMEM(pair, F32),
            pltpu.VMEM(pair, F32),
            pltpu.VMEM((2, *pair), BF),
            pltpu.VMEM((2, *pair), BF),
            pltpu.SemaphoreType.DMA((GATHER_SENDS,)),
            pltpu.SemaphoreType.DMA((2, 4 * RING)),
            pltpu.SemaphoreType.DMA((2, RING)),
            pltpu.SemaphoreType.DMA((4,)),
            pltpu.SemaphoreType.DMA((2,)),
        ],
        compiler_params=pltpu.CompilerParams(
            collective_id=0, has_side_effects=True, vmem_limit_bytes=32 << 20
        ),
    )(in_codes, out_codes, tokens, upstream, wi, wo)


def panel_kernel(in_codes, out_codes, act, gh, wi, wo, parts, lay, inp):
    lay[...] = jnp.zeros_like(lay)
    inp[...] = jnp.zeros_like(inp)

    def outward(k, _):
        i, j, filled = split_code(in_codes, k)

        @pl.when(filled)
        def _():
            inp[i] += dot(gh[j], wi[k], ((1,), (1,)))

        i2, j2, filled2 = split_code(out_codes, k)

        @pl.when(filled2)
        def _():
            lay[i2] += dot(act[j2], wo[k], ((1,), (0,)))

        return 0

    lax.fori_loop(0, wi.shape[0], outward, 0)
    rows, width = parts.shape[-2:]

    def round_up(i, _):
        for t, total in enumerate((lay, inp)):
            full = total[i].astype(BF)
            for core in range(2):
                for lo in range(2):
                    parts[core, i % RING, lo, i // RING, t] = full[
                        lo * rows : (lo + 1) * rows, core * width : (core + 1) * width
                    ]
        return 0

    lax.fori_loop(0, lay.shape[0], round_up, 0)


def panel(in_codes, out_codes, act, gh, wi, wo, rows):
    vmem, smem = specs()
    size = wi.shape[-1]
    total = pltpu.VMEM((2 * RING, 2 * rows, size), F32)
    return pl.pallas_call(
        panel_kernel,
        name="panel",
        out_shape=jax.ShapeDtypeStruct((2, RING, 2, 2, 2, rows, size // 2), BF),
        in_specs=[smem, smem, vmem, vmem, vmem, vmem],
        out_specs=vmem,
        scratch_shapes=[total, total],
        compiler_params=pltpu.CompilerParams(vmem_limit_bytes=32 << 20),
    )(in_codes, out_codes, act, gh, wi, wo)


REDUCE_SENDS = 48


def reduce_kernel(
    in_codes, out_codes, x, act, gh, parts, layer, grad_tokens, grad_in, grad_out,
    pair_buf, y_far, y_buf, z_far, z_buf, hi_sum, hi_buf, lo_sum, lo_buf,
    send_sems, pair_sems, y_sems, z_sems, end_sems,
):
    at = Place()
    peers = at.peers()
    meet(peers)
    out = Sender(send_sems, peers)
    half = RING // 2
    marks, signs = ("+", "-"), (1, -1)

    def wide(value):
        return value.astype(F32)

    def y_of(dist):
        return lax.rem(at.y + dist + RING, RING)

    def z_of(dist):
        return lax.rem(at.z + dist + RING, RING)

    def share(t, k):
        if t == 0:
            i, j, filled = split_code(in_codes, k)
            product = dot(token_tile(x, 0, i), gh[j], ((0,), (0,)))
        else:
            i, j, filled = split_code(out_codes, k)
            product = dot(act[j], token_tile(x, 1, i), ((0,), (0,)))
        return jnp.where(filled, product, 0.0)

    def chip(y, lo):
        return wide(parts[at.core, y, lo]) + wide(pair_buf[y, lo])

    order = [half] + [sign * dist for dist in range(half - 1, 0, -1) for sign in signs] + [0]
    for dist in order:
        y = y_of(dist)
        out.copy(parts.at[1 - at.core, y], pair_buf.at[y], pair_sems.at[y], "core")
    for d in range(2):
        z_far[d] = share(d, z_of(half)).astype(BF)
        out.copy(z_far.at[d], z_buf.at[d, 0, d], z_sems.at[d, 0, d], "z" + marks[d])
    y = y_of(half)
    out.arrived(pair_buf.at[y], pair_sems.at[y])
    for d in range(2):
        y_far[d] = chip(y, d).astype(BF)
        out.copy(y_far.at[d], y_buf.at[d, 0, d], y_sems.at[d, 0, d], "y" + marks[d])

    for step in range(1, half):
        for d in range(2):
            y = y_of(signs[d] * (half - step))
            out.arrived(pair_buf.at[y], pair_sems.at[y])
            for lo in (d, 1 - d):
                value = chip(y, lo)
                slot = y_buf.at[d, step - 1, lo]
                if step > 1 or lo == d:
                    out.arrived(slot, y_sems.at[d, step - 1, lo])
                    value = value + wide(slot[...])
                slot[...] = value.astype(BF)
                out.copy(slot, y_buf.at[d, step, lo], y_sems.at[d, step, lo], "y" + marks[d])
        for d in range(2):
            k = z_of(signs[d] * (half - step))
            for t in (d, 1 - d):
                value = share(t, k)
                slot = z_buf.at[d, step - 1, t]
                if step > 1 or t == d:
                    out.arrived(slot, z_sems.at[d, step - 1, t])
                    value = value + wide(slot[...])
                slot[...] = value.astype(BF)
                out.copy(slot, z_buf.at[d, step, t], z_sems.at[d, step, t], "z" + marks[d])

    out.arrived(pair_buf.at[at.y], pair_sems.at[at.y])
    for lo in range(2):
        for d in range(2):
            out.arrived(y_buf.at[d, half - 1, lo], y_sems.at[d, half - 1, lo])

    def y_total(lo, hi):
        value = wide(parts[at.core, at.y, lo, hi]) + wide(pair_buf[at.y, lo, hi])
        return value + wide(y_buf[0, half - 1, lo, hi]) + wide(y_buf[1, half - 1, lo, hi])

    for lo in range(2):
        hi_sum[lo] = y_total(lo, 1 - at.hi).astype(BF)
    out.copy(hi_sum, hi_buf, end_sems.at[0], "hi")
    own = [share(t, at.z) for t in range(2)]
    out.arrived(hi_buf, end_sems.at[0])
    lo_sum[...] = (y_total(1 - at.lo, at.hi) + wide(hi_buf[1 - at.lo])).astype(BF)
    out.copy(lo_sum, lo_buf, end_sems.at[1], "lo")
    for t, result in enumerate((grad_in, grad_out)):
        value = own[t]
        for d in range(2):
            slot = z_buf.at[d, half - 1, t]
            out.arrived(slot, z_sems.at[d, half - 1, t])
            value = value + wide(slot[...])
        result[...] = value.astype(BF)
    out.arrived(lo_buf, end_sems.at[1])
    total = y_total(at.lo, at.hi) + wide(hi_buf[at.lo]) + wide(lo_buf[...])
    layer[...] = total[0].astype(BF)
    grad_tokens[...] = total[1].astype(BF)
    out.drain()


def reduce(in_codes, out_codes, x, act, gh, parts):
    vmem, smem = specs()
    rows, width = parts.shape[-2:]
    size = act.shape[-1]
    half = RING // 2
    block, tile = (2, rows, width), (size, size)
    return pl.pallas_call(
        reduce_kernel,
        name="reduce_all",
        out_shape=(
            jax.ShapeDtypeStruct((rows, width), BF),
            jax.ShapeDtypeStruct((rows, width), BF),
            jax.ShapeDtypeStruct(tile, BF),
            jax.ShapeDtypeStruct(tile, BF),
        ),
        in_specs=[smem, smem, vmem, vmem, vmem, vmem],
        out_specs=(vmem,) * 4,
        scratch_shapes=[
            pltpu.VMEM((RING, 2, 2, *block), BF),
            pltpu.VMEM((2, 2, *block), BF),
            pltpu.VMEM((2, half, 2, 2, *block), BF),
            pltpu.VMEM((2, *tile), BF),
            pltpu.VMEM((2, half, 2, *tile), BF),
            pltpu.VMEM((2, *block), BF),
            pltpu.VMEM((2, *block), BF),
            pltpu.VMEM(block, BF),
            pltpu.VMEM(block, BF),
            pltpu.SemaphoreType.DMA((REDUCE_SENDS,)),
            pltpu.SemaphoreType.DMA((RING,)),
            pltpu.SemaphoreType.DMA((2, half, 2)),
            pltpu.SemaphoreType.DMA((2, half, 2)),
            pltpu.SemaphoreType.DMA((2,)),
        ],
        compiler_params=pltpu.CompilerParams(
            collective_id=1, has_side_effects=True, vmem_limit_bytes=32 << 20
        ),
    )(in_codes, out_codes, x, act, gh, parts)


def per_device(tokens, upstream, w_in, in_codes, w_out, out_codes):
    lo = lax.axis_index("row") % 2
    in_codes, out_codes = (
        lax.dynamic_index_in_dim(codes.reshape(RING, 2), lo, axis=1, keepdims=False)
        for codes in (in_codes, out_codes)
    )
    x, wi, wo, act, gh = gather(in_codes, out_codes, tokens, upstream, w_in[0, 0], w_out[0, 0])
    parts = panel(in_codes, out_codes, act, gh, wi, wo, tokens.shape[0])
    layer, grad_tokens, grad_in, grad_out = reduce(in_codes, out_codes, x, act, gh, parts)
    return layer, grad_tokens, grad_in[None, None], grad_out[None, None]


def solution(mesh):
    placed = (
        P("row", "col"),
        P("row", "col"),
        P("col", "row", None, None),
        P("col", None),
        P("col", "row", None, None),
        P("col", None),
    )
    return jax.shard_map(
        per_device,
        mesh=mesh,
        in_specs=placed,
        out_specs=(
            P("row", "col"),
            P("row", "col"),
            P("col", "row", None, None),
            P("col", "row", None, None),
        ),
        check_vma=False,
    )
```

time: 394 us -> 113 us (0.29)
  the two profiles are of different devices: /device:TPU:1 before, /device:TPU:58 now
where the time goes in v3:
time: 113 us
  Pallas kernels  103 us (91%)
  local copies, waits for them, and re-layouts  6.76 us (6%)
  other arithmetic  2.64 us (2%)
    pallas_call x1, Pallas kernels, gather(): pl.pallas_call(gather_kernel, name='gather_all', out_shape=(jax.ShapeDtyp...  57.3 us
    pallas_call x1, Pallas kernels, reduce(): pl.pallas_call(reduce_kernel, name='reduce_all', out_shape=(jax.ShapeDtyp...  43.2 us
    unnamed x13, local copies, waits for them, and re-layouts  6.38 us
    unnamed x2, other arithmetic  2.64 us
    pallas_call x1, Pallas kernels, panel(): pl.pallas_call(panel_kernel, name='panel', out_shape=jax.ShapeDtypeStruct...  2.42 us

profile of v3, /device:TPU:58, one launch (start us, length us, event | category | flops | bytes accessed | tf_op | source)
XLA Modules:
  0.0 113.0 jit_solution(15960761282079720537)
XLA Ops:
  0.6 0.5 broadcast.9
  1.2 1.3 %reduce.10 = s32[16]{0:T(128)S(1)} reduce(s32[1,16]{1,0:T(1,128)} %param.9, s32[]{:T(128)} %broadcast.9), dimensions={0}, to_apply=%param.9.reduce_sub_computation.3 | reduce | bytes 132 | tf_op args[3]
  2.5 1.3 %reduce.11 = s32[16]{0:T(128)S(1)} reduce(s32[1,16]{1,0:T(1,128)} %param.11, s32[]{:T(128)} %broadcast.9), dimensions={0}, to_apply=%param.11.reduce_sub_computation.3 | reduce | bytes 132 | tf_op args[5]
  3.8 0.1 reshape.15
  3.9 0.1 reshape.14
  4.0 0.2 dynamic-slice_reduce_fusion
  4.2 0.0 copy-start
  4.2 0.9 copy-done
  5.1 0.0 copy-start.1
  5.1 0.9 copy-done.1
  6.0 0.0 copy-start.2
  6.0 0.8 copy-done.2
  6.8 0.0 copy-start.3
  6.8 0.8 copy-done.3
  7.5 57.3 %gather_all.1 = (bf16[2,32,2,128,128]{4,3,2,1,0:T(8,128)(2,1)S(1)}, bf16[8,256,256]{2,1,0:T(8,128)(2,1)S(1)}, bf16[8,256,256]{2,1,0:T(8,128)(2,1)S(1)}, bf16[2,2...) custom-call(s32[8]{0:T(128)S(1)} %get-tuple-element.23.in_codes, s32[8]{0:T(128)S(1)} %get-tuple-element.22.out_codes, ...), custom_call_target="tpu_custom_call" | custom-call | tf_op jit(solution)/shard_map/gather_all/pallas_call | solution.py:195
  64.8 2.4 %panel.1.parts = bf16[2,8,2,2,2,128,128]{6,5,4,3,2,1,0:T(8,128)(2,1)S(1)} custom-call(s32[8]{0:T(128)S(1)} %get-tuple-element.23.in_codes, s32[8]{0:T(128)S(1)} %get-tuple-element.22.out_codes, bf16[2,256,256]{2,1,0:T(8,128)(2,1)S(1)} %get-tuple-element.14.act, bf16[2,256,256]{2,1,0:T(8,128)(2,1)S(1)} %get-tuple-element.15.gh, ...), custom_call_target="tpu_custom_call" | custom-call | tf_op jit(solution)/shard_map/panel/pallas_call | solution.py:263
  67.2 43.2 %reduce_all.1 = (bf16[128,128]{1,0:T(8,128)(2,1)S(1)}, bf16[128,128]{1,0:T(8,128)(2,1)S(1)}, bf16[256,256]{1,0:T(8,128)(2,1)S(1)}, bf16[256,256]{1,0:T(8,128)(2,1)S(1)}) custom-call(s32[8]{0:T(128)S(1)} %get-tuple-element.23.in_codes, s32[8]{0:T(128)S(1)} %get-tuple-element.22.out_codes, bf16[2,32,2,128,128]{4,3,2,1,0:T(8,128)(2,1)S(1)} %get-tuple-element.13.x, ...), custom_call_target="tpu_custom_call" | custom-call | tf_op jit(solution)/shard_map/reduce_all/pallas_call | solution.py:382
  110.4 0.6 copy.14
  111.0 0.6 copy.15
  111.7 0.7 copy.16
  112.3 0.7 copy.17
Async XLA Ops:
  4.2 0.9 copy-start
  5.1 0.9 copy-start.1
  6.0 0.8 copy-start.2
  6.8 0.8 copy-start.3

commit v4 on v3

--- a/solution.py
+++ b/solution.py
@@ -32,6 +32,7 @@
             "y+": (self.row, self.col_at(1)),
             "y-": (self.row, self.col_at(-1)),
             "hi": (self.row, self.col_at(0, 1 - self.hi)),
+            "diag": (self.row_at(0, 1 - self.lo), self.col_at(0, 1 - self.hi)),
             "core": (self.row, self.col_at(0, None, 1 - self.core)),
         }
 
@@ -82,7 +83,7 @@
 
 
 def split_code(ref, k):
-    code = ref[k]
+    code = ref[2 * k + lax.axis_index("row") % 2]
     clipped = jnp.maximum(code, 0)
     return clipped // 2, clipped % 2, code >= 0
 
@@ -129,23 +130,26 @@
         out.arrived(held[t].at[z], w_sems.at[t, z])
         w_send(t, z, *to)
 
-    x_send(at.lo, at.col, "lo", "hi", "y+", "y-")
+    x_send(at.lo, at.col, "y+", "y-", "lo", "diag", "hi")
     for t in range(2):
         w_send(t, at.z, "z+", "z-")
     x_send(at.lo, at.col, "core")
-    x_pass(1 - at.lo, at.col, "hi", "y+", "y-", "core")
+    x_pass(1 - at.lo, at.col, "y+", "y-", "core")
     x_pass(at.lo, at.col_at(0, 1 - at.hi), "y+", "y-", "core")
     x_pass(1 - at.lo, at.col_at(0, 1 - at.hi), "y+", "y-", "core")
     half = RING // 2
     flows = ((-1, "+"), (1, "-"))
+    kinds = ((at.lo, at.hi), (1 - at.lo, at.hi), (at.lo, 1 - at.hi), (1 - at.lo, 1 - at.hi))
     for step in range(1, half + 1):
-        for d, (sign, mark) in enumerate(flows):
-            for n, (lo, hi) in enumerate(((at.lo, at.hi), (1 - at.lo, at.hi), (at.lo, 1 - at.hi), (1 - at.lo, 1 - at.hi))):
+        for n, (lo, hi) in enumerate(kinds):
+            for d, (sign, mark) in enumerate(flows):
                 if step == half and n % 2 != d:
                     continue
                 onward = step < half - 1 or (step == half - 1 and n % 2 == d)
                 x_pass(lo, at.col_at(sign * step, hi), *(("y" + mark,) if onward else ()), "core")
-        for t in range(2):
+            if n % 2 == 1:
+                continue
+            t = n // 2
             for d, (sign, mark) in enumerate(flows):
                 if step == half and t != d:
                     continue
@@ -202,7 +206,7 @@
             jax.ShapeDtypeStruct(pair, BF),
             jax.ShapeDtypeStruct(pair, BF),
         ),
-        in_specs=[smem, smem, vmem, vmem, vmem, vmem],
+        in_specs=[smem, smem] + [pl.BlockSpec(memory_space=pltpu.HBM)] * 4,
         out_specs=(vmem,) * 5,
         scratch_shapes=[
             pltpu.VMEM(pair, F32),
@@ -276,7 +280,7 @@
 
 def reduce_kernel(
     in_codes, out_codes, x, act, gh, parts, layer, grad_tokens, grad_in, grad_out,
-    pair_buf, y_far, y_buf, z_far, z_buf, hi_sum, hi_buf, lo_sum, lo_buf,
+    pair_buf, y_far, y_buf, z_far, z_buf, end_sum, end_buf,
     send_sems, pair_sems, y_sems, z_sems, end_sems,
 ):
     at = Place()
@@ -320,30 +324,37 @@
         y_far[d] = chip(y, d).astype(BF)
         out.copy(y_far.at[d], y_buf.at[d, 0, d], y_sems.at[d, 0, d], "y" + marks[d])
 
+    def y_hop(step, d, lo):
+        y = y_of(signs[d] * (half - step))
+        value = chip(y, lo)
+        slot = y_buf.at[d, step - 1, lo]
+        if step > 1 or lo == d:
+            out.arrived(slot, y_sems.at[d, step - 1, lo])
+            value = value + wide(slot[...])
+        slot[...] = value.astype(BF)
+        out.copy(slot, y_buf.at[d, step, lo], y_sems.at[d, step, lo], "y" + marks[d])
+
+    def z_hop(step, d, t):
+        value = share(t, z_of(signs[d] * (half - step)))
+        slot = z_buf.at[d, step - 1, t]
+        if step > 1 or t == d:
+            out.arrived(slot, z_sems.at[d, step - 1, t])
+            value = value + wide(slot[...])
+        slot[...] = value.astype(BF)
+        out.copy(slot, z_buf.at[d, step, t], z_sems.at[d, step, t], "z" + marks[d])
+
     for step in range(1, half):
         for d in range(2):
             y = y_of(signs[d] * (half - step))
             out.arrived(pair_buf.at[y], pair_sems.at[y])
-            for lo in (d, 1 - d):
-                value = chip(y, lo)
-                slot = y_buf.at[d, step - 1, lo]
-                if step > 1 or lo == d:
-                    out.arrived(slot, y_sems.at[d, step - 1, lo])
-                    value = value + wide(slot[...])
-                slot[...] = value.astype(BF)
-                out.copy(slot, y_buf.at[d, step, lo], y_sems.at[d, step, lo], "y" + marks[d])
-        for d in range(2):
-            k = z_of(signs[d] * (half - step))
-            for t in (d, 1 - d):
-                value = share(t, k)
-                slot = z_buf.at[d, step - 1, t]
-                if step > 1 or t == d:
-                    out.arrived(slot, z_sems.at[d, step - 1, t])
-                    value = value + wide(slot[...])
-                slot[...] = value.astype(BF)
-                out.copy(slot, z_buf.at[d, step, t], z_sems.at[d, step, t], "z" + marks[d])
+        for n in (1, 0) if step == 1 else (0, 1):
+            for d in range(2):
+                y_hop(step, d, d if n == 0 else 1 - d)
+            for d in range(2):
+                z_hop(step, d, d if n == 0 else 1 - d)
 
     out.arrived(pair_buf.at[at.y], pair_sems.at[at.y])
+    own = [share(t, at.z) for t in range(2)]
     for lo in range(2):
         for d in range(2):
             out.arrived(y_buf.at[d, half - 1, lo], y_sems.at[d, half - 1, lo])
@@ -352,13 +363,10 @@
         value = wide(parts[at.core, at.y, lo, hi]) + wide(pair_buf[at.y, lo, hi])
         return value + wide(y_buf[0, half - 1, lo, hi]) + wide(y_buf[1, half - 1, lo, hi])
 
-    for lo in range(2):
-        hi_sum[lo] = y_total(lo, 1 - at.hi).astype(BF)
-    out.copy(hi_sum, hi_buf, end_sems.at[0], "hi")
-    own = [share(t, at.z) for t in range(2)]
-    out.arrived(hi_buf, end_sems.at[0])
-    lo_sum[...] = (y_total(1 - at.lo, at.hi) + wide(hi_buf[1 - at.lo])).astype(BF)
-    out.copy(lo_sum, lo_buf, end_sems.at[1], "lo")
+    ends = (("hi", at.lo, 1 - at.hi), ("diag", 1 - at.lo, 1 - at.hi), ("lo", 1 - at.lo, at.hi))
+    for n, (peer, lo, hi) in enumerate(ends):
+        end_sum[n] = y_total(lo, hi).astype(BF)
+        out.copy(end_sum.at[n], end_buf.at[n], end_sems.at[n], peer)
     for t, result in enumerate((grad_in, grad_out)):
         value = own[t]
         for d in range(2):
@@ -366,11 +374,34 @@
             out.arrived(slot, z_sems.at[d, half - 1, t])
             value = value + wide(slot[...])
         result[...] = value.astype(BF)
-    out.arrived(lo_buf, end_sems.at[1])
-    total = y_total(at.lo, at.hi) + wide(hi_buf[at.lo]) + wide(lo_buf[...])
+    total = y_total(at.lo, at.hi)
+    for n in (2, 1, 0):
+        out.arrived(end_buf.at[n], end_sems.at[n])
+        total = total + wide(end_buf[n])
     layer[...] = total[0].astype(BF)
     grad_tokens[...] = total[1].astype(BF)
     out.drain()
+
+
+def write_kernel(*refs):
+    sems = refs[-1]
+    count = len(refs) // 2
+    copies = [pltpu.make_async_copy(refs[n], refs[count + n], sems.at[n]) for n in range(count)]
+    for copy in copies:
+        copy.start()
+    for copy in copies:
+        copy.wait()
+
+
+def write(*values):
+    return pl.pallas_call(
+        write_kernel,
+        name="write_all",
+        out_shape=tuple(jax.ShapeDtypeStruct(v.shape, v.dtype) for v in values),
+        in_specs=[pl.BlockSpec(memory_space=pltpu.VMEM)] * len(values),
+        out_specs=(pl.BlockSpec(memory_space=pltpu.HBM),) * len(values),
+        scratch_shapes=[pltpu.SemaphoreType.DMA((len(values),))],
+    )(*values)
 
 
 def reduce(in_codes, out_codes, x, act, gh, parts):
@@ -396,15 +427,13 @@
             pltpu.VMEM((2, half, 2, 2, *block), BF),
             pltpu.VMEM((2, *tile), BF),
             pltpu.VMEM((2, half, 2, *tile), BF),
-            pltpu.VMEM((2, *block), BF),
-            pltpu.VMEM((2, *block), BF),
-            pltpu.VMEM(block, BF),
-            pltpu.VMEM(block, BF),
+            pltpu.VMEM((3, *block), BF),
+            pltpu.VMEM((3, *block), BF),
             pltpu.SemaphoreType.DMA((REDUCE_SENDS,)),
             pltpu.SemaphoreType.DMA((RING,)),
             pltpu.SemaphoreType.DMA((2, half, 2)),
             pltpu.SemaphoreType.DMA((2, half, 2)),
-            pltpu.SemaphoreType.DMA((2,)),
+            pltpu.SemaphoreType.DMA((3,)),
         ],
         compiler_params=pltpu.CompilerParams(
             collective_id=1, has_side_effects=True, vmem_limit_bytes=32 << 20
@@ -413,14 +442,11 @@
 
 
 def per_device(tokens, upstream, w_in, in_codes, w_out, out_codes):
-    lo = lax.axis_index("row") % 2
-    in_codes, out_codes = (
-        lax.dynamic_index_in_dim(codes.reshape(RING, 2), lo, axis=1, keepdims=False)
-        for codes in (in_codes, out_codes)
-    )
+    in_codes, out_codes = in_codes[0], out_codes[0]
     x, wi, wo, act, gh = gather(in_codes, out_codes, tokens, upstream, w_in[0, 0], w_out[0, 0])
     parts = panel(in_codes, out_codes, act, gh, wi, wo, tokens.shape[0])
-    layer, grad_tokens, grad_in, grad_out = reduce(in_codes, out_codes, x, act, gh, parts)
+    results = reduce(in_codes, out_codes, x, act, gh, parts)
+    layer, grad_tokens, grad_in, grad_out = write(*results)
     return layer, grad_tokens, grad_in[None, None], grad_out[None, None]
 
 

time: 113 us -> 106 us (0.938)
  the two profiles are of different devices: /device:TPU:58 before, /device:TPU:1 now
where the time goes in v4:
time: 106 us; the launch traced here: 105 us
  Pallas kernels  97.7 us (92%)
  local copies, waits for them, and re-layouts  7.12 us (7%)
    pallas_call x1, Pallas kernels, gather(): pl.pallas_call(gather_kernel, name='gather_all', out_shape=(jax.ShapeDtyp...  56.2 us
    pallas_call x1, Pallas kernels, reduce(): pl.pallas_call(reduce_kernel, name='reduce_all', out_shape=(jax.ShapeDtyp...  35.7 us
    unnamed x20, local copies, waits for them, and re-layouts  7.12 us
    pallas_call x1, Pallas kernels, panel(): pl.pallas_call(panel_kernel, name='panel', out_shape=jax.ShapeDtypeStruct...  4.03 us

profile of v4, /device:TPU:1, one launch (start us, length us, event | category | flops | bytes accessed | tf_op | source)
XLA Modules:
  0.0 105.5 jit_solution(13045514767341710018)
XLA Ops:
  0.6 0.0 copy-start
  0.6 0.9 copy-done
  1.5 0.0 copy-start.1
  1.5 0.9 copy-done.1
  2.4 0.0 copy-start.4
  2.4 0.8 copy-done.4
  3.2 0.0 copy-start.5
  3.2 0.8 copy-done.5
  4.0 0.0 copy-start.8
  4.0 0.7 copy-done.8
  4.6 0.0 copy-start.9
  4.6 0.7 copy-done.9
  5.3 56.2 %gather_all.1 = (bf16[2,32,2,128,128]{4,3,2,1,0:T(8,128)(2,1)S(1)}, bf16[8,256,256]{2,1,0:T(8,128)(2,1)S(1)}, bf16[8,256,256]{2,1,0:T(8,128)(2,1)S(1)}, bf16[2,2...) custom-call(s32[16]{0:T(128)S(1)} %bitcast.8, s32[16]{0:T(128)S(1)} %bitcast.11, bf16[128,128]{1,0:T(8,128)(2,1)S(1)} %copy-done.4, ...), custom_call_target="tpu_custom_call" | custom-call | tf_op jit(solution)/shard_map/gather_all/pallas_call | solution.py:199
  61.4 4.0 %panel.1.parts = bf16[2,8,2,2,2,128,128]{6,5,4,3,2,1,0:T(8,128)(2,1)S(1)} custom-call(s32[16]{0:T(128)S(1)} %bitcast.9, s32[16]{0:T(128)S(1)} %bitcast.12, bf16[2,256,256]{2,1,0:T(8,128)(2,1)S(1)} %get-tuple-element.18.act, bf16[2,256,256]{2,1,0:T(8,128)(2,1)S(1)} %get-tuple-element.19.gh, bf16[8,256,256]{2,1,0:T(8,128)(2,1)S(1)} %get-tuple-element.20.wi, ...), custom_call_target="tpu_custom_call" | custom-call | tf_op jit(solution)/shard_map/panel/pallas_call | solution.py:267
  65.5 35.7 %reduce_all.1 = (bf16[128,128]{1,0:T(8,128)(2,1)S(1)}, bf16[128,128]{1,0:T(8,128)(2,1)S(1)}, bf16[256,256]{1,0:T(8,128)(2,1)S(1)}, bf16[256,256]{1,0:T(8,128)(2,1)S(1)}) custom-call(s32[16]{0:T(128)S(1)} %bitcast.10, s32[16]{0:T(128)S(1)} %bitcast.13, bf16[2,32,2,128,128]{4,3,2,1,0:T(8,128)(2,1)S(1)} %get-tuple-element.17.x, ...), custom_call_target="tpu_custom_call" | custom-call | tf_op jit(solution)/shard_map/reduce_all/pallas_call | solution.py:413
  101.2 0.0 copy-start.2
  101.2 0.6 copy-done.2
  101.9 0.0 copy-start.3
  101.9 0.6 copy-done.3
  102.5 0.0 copy-start.6
  102.5 0.6 copy-done.6
  103.1 0.0 copy-start.7
  103.1 0.6 copy-done.7
  103.7 1.8 %write_all.1 = (bf16[128,128]{1,0:T(8,128)(2,1)}, bf16[128,128]{1,0:T(8,128)(2,1)}, bf16[256,256]{1,0:T(8,128)(2,1)}, bf16[256,256]{1,0:T(8,128)(2,1)}) custom-call(bf16[128,128]{1,0:T(8,128)(2,1)} %copy-done.6, bf16[128,128]{1,0:T(8,128)(2,1)} %copy-done.7, bf16[256,256]{1,0:T(8,128)(2,1)} %copy-done.2, bf16[256,256]{1,0:T(8,128)(2,1)} %copy-done.3), custom_call_target="tpu_custom_call" | custom-call | tf_op jit(solution)/shard_map/write_all/pallas_call | solution.py:397
Async XLA Ops:
  0.6 0.9 copy-start
  1.5 0.9 copy-start.1
  2.4 0.8 copy-start.4
  3.2 0.8 copy-start.5
  4.0 0.7 copy-start.8
  4.6 0.7 copy-start.9
  101.2 0.7 copy-start.2
  101.9 0.6 copy-start.3
  102.5 0.6 copy-start.6
  103.1 0.6 copy-start.7

commit v5 on v4

v5 whole, which is shorter than its diff:
```python
import jax
import jax.numpy as jnp
from jax import lax
from jax.experimental import pallas as pl
from jax.experimental.pallas import tpu as pltpu
from jax.sharding import PartitionSpec as P

RING = 8
BF, F32 = jnp.bfloat16, jnp.float32


class Place:
    def __init__(self):
        row, col = lax.axis_index("row"), lax.axis_index("col")
        self.row, self.col = row, col
        self.z, self.lo = row // 2, row % 2
        self.hi, self.y, self.core = col // (2 * RING), (col // 2) % RING, col % 2

    def row_at(self, dz=0, lo=None):
        return lax.rem(self.z + dz + RING, RING) * 2 + (self.lo if lo is None else lo)

    def col_at(self, dy=0, hi=None, core=None):
        y = lax.rem(self.y + dy + RING, RING)
        hi = self.hi if hi is None else hi
        return (hi * RING + y) * 2 + (self.core if core is None else core)

    def peers(self):
        return {
            "z+": (self.row_at(1), self.col),
            "z-": (self.row_at(-1), self.col),
            "lo": (self.row_at(0, 1 - self.lo), self.col),
            "y+": (self.row, self.col_at(1)),
            "y-": (self.row, self.col_at(-1)),
            "hi": (self.row, self.col_at(0, 1 - self.hi)),
            "diag": (self.row_at(0, 1 - self.lo), self.col_at(0, 1 - self.hi)),
            "core": (self.row, self.col_at(0, None, 1 - self.core)),
        }


def meet(peers):
    barrier = pltpu.get_barrier_semaphore()
    for device in peers.values():
        pl.semaphore_signal(barrier, inc=1, device_id=device, device_id_type=pl.DeviceIdType.MESH)
    pl.semaphore_wait(barrier, len(peers))


class Sender:
    def __init__(self, sems, peers):
        self.sems, self.peers, self.started = sems, peers, []

    def copy(self, src, dst, recv_sem, peer):
        copy = pltpu.make_async_remote_copy(
            src_ref=src,
            dst_ref=dst,
            send_sem=self.sems.at[len(self.started)],
            recv_sem=recv_sem,
            device_id=self.peers[peer],
            device_id_type=pl.DeviceIdType.MESH,
        )
        copy.start()
        self.started.append(copy)

    def arrived(self, dst, recv_sem):
        pltpu.make_async_remote_copy(
            src_ref=dst,
            dst_ref=dst,
            send_sem=self.sems.at[0],
            recv_sem=recv_sem,
            device_id=self.peers["core"],
            device_id_type=pl.DeviceIdType.MESH,
        ).wait_recv()

    def drain(self):
        for copy in self.started:
            copy.wait_send()


def dot(a, b, contract):
    return lax.dot_general(a, b, (contract, ((), ())), preferred_element_type=F32)


def split_code(ref, k):
    code = ref[2 * k + lax.axis_index("row") % 2]
    clipped = jnp.maximum(code, 0)
    return clipped // 2, clipped % 2, code >= 0


def token_tile(x, which, i):
    halves = [jnp.concatenate([x[lo, 2 * i, which], x[lo, 2 * i + 1, which]], axis=1) for lo in range(2)]
    return jnp.concatenate(halves, axis=0)


SENDS = 144


def whole_kernel(
    in_codes, out_codes, tokens, upstream, wi_ref, wo_ref, layer, grad_tokens, grad_in, grad_out,
    xg, wig, wog, hid, gact, mine, theirs, act, gh, slot_of,
    parts, pair_buf, y_far, y_buf, z_far, z_buf, end_sum, end_buf,
    send_sems, x_sems, w_sems, own_sems, swap_sems, pair_sems, y_sems, z_sems, end_sems,
):
    at = Place()
    peers = at.peers()
    x_own = xg.at[at.lo, at.col]
    own = [
        pltpu.make_async_copy(tokens, x_own.at[0], own_sems.at[0]),
        pltpu.make_async_copy(upstream, x_own.at[1], own_sems.at[1]),
        pltpu.make_async_copy(wi_ref, wig.at[at.z], own_sems.at[2]),
        pltpu.make_async_copy(wo_ref, wog.at[at.z], own_sems.at[3]),
    ]
    for copy in own:
        copy.start()
    meet(peers)
    out = Sender(send_sems, peers)
    for copy in own:
        copy.wait()
    held = (wig, wog)

    def x_send(lo, col, *to):
        for peer in to:
            out.copy(xg.at[lo, col], xg.at[lo, col], x_sems.at[lo, col], peer)

    def x_pass(lo, col, *to):
        out.arrived(xg.at[lo, col], x_sems.at[lo, col])
        x_send(lo, col, *to)

    def w_send(t, z, *to):
        for peer in to:
            out.copy(held[t].at[z], held[t].at[z], w_sems.at[t, z], peer)

    def w_pass(t, z, *to):
        out.arrived(held[t].at[z], w_sems.at[t, z])
        w_send(t, z, *to)

    x_send(at.lo, at.col, "y+", "y-", "lo", "diag", "hi")
    for t in range(2):
        w_send(t, at.z, "z+", "z-")
    x_send(at.lo, at.col, "core")
    x_pass(1 - at.lo, at.col, "y+", "y-", "core")
    x_pass(at.lo, at.col_at(0, 1 - at.hi), "y+", "y-", "core")
    x_pass(1 - at.lo, at.col_at(0, 1 - at.hi), "y+", "y-", "core")
    half = RING // 2
    flows = ((-1, "+"), (1, "-"))
    kinds = ((at.lo, at.hi), (1 - at.lo, at.hi), (at.lo, 1 - at.hi), (1 - at.lo, 1 - at.hi))
    for step in range(1, half + 1):
        for n, (lo, hi) in enumerate(kinds):
            for d, (sign, mark) in enumerate(flows):
                if step == half and n % 2 != d:
                    continue
                onward = step < half - 1 or (step == half - 1 and n % 2 == d)
                x_pass(lo, at.col_at(sign * step, hi), *(("y" + mark,) if onward else ()), "core")
            if n % 2 == 1:
                continue
            t = n // 2
            for d, (sign, mark) in enumerate(flows):
                if step == half and t != d:
                    continue
                onward = step < half - 1 or (step == half - 1 and t == d)
                w_pass(t, lax.rem(at.z + sign * step + RING, RING), *(("z" + mark,) if onward else ()))
    for step in range(RING):
        for hi in range(2):
            for lo in range(2):
                col = at.col_at(step, hi, 1 - at.core)
                out.arrived(xg.at[lo, col], x_sems.at[lo, col])

    hid[...] = jnp.zeros_like(hid)
    gact[...] = jnp.zeros_like(gact)

    def inward(codes, which, weights, total, contract):
        def one(k, _):
            i, j, filled = split_code(codes, k)
            product = dot(token_tile(xg, which, i), weights[k], contract)
            for col in range(2):
                total[col] += jnp.where(jnp.logical_and(filled, j == col), product, 0.0)
            return 0

        lax.fori_loop(0, RING, one, 0, unroll=True)
        mine[which] = total[...].astype(BF)
        out.copy(mine.at[which], theirs.at[which], swap_sems.at[which], "lo")

    inward(in_codes, 0, wig, hid, ((1,), (0,)))
    inward(out_codes, 1, wog, gact, ((1,), (1,)))

    def slot_at(code, _):
        for t, codes in enumerate((in_codes, out_codes)):
            slot = jnp.int32(-1)
            for k in range(RING):
                slot = jnp.where(codes[2 * k + at.lo] == code, k, slot)
            slot_of[t, code] = slot
        return 0

    lax.fori_loop(0, 4 * RING, slot_at, 0)

    marks, signs = ("+", "-"), (1, -1)
    size = hid.shape[-1]
    width = size // 2

    def wide(value):
        return value.astype(F32)

    def y_of(dist):
        return lax.rem(at.y + dist + RING, RING)

    def z_of(dist):
        return lax.rem(at.z + dist + RING, RING)

    def share(t, k):
        if t == 0:
            i, j, filled = split_code(in_codes, k)
            product = dot(token_tile(xg, 0, i), gh[j], ((0,), (0,)))
        else:
            i, j, filled = split_code(out_codes, k)
            product = dot(act[j], token_tile(xg, 1, i), ((0,), (0,)))
        return jnp.where(filled, product, 0.0)

    order = [half] + [sign * dist for dist in range(half - 1, 0, -1) for sign in signs] + [0]

    def make(t):
        left, weights, contract = ((act, wog, ((1,), (0,))), (gh, wig, ((1,), (1,))))[t]
        for dist in order:
            y = y_of(dist)
            for hi in range(2):
                full = jnp.zeros((size, size), F32)
                for j in range(2):
                    slot = slot_of[1 - t, 2 * (hi * RING + y) + j]
                    product = dot(left[j], weights[jnp.maximum(slot, 0)], contract)
                    full = full + jnp.where(slot >= 0, product, 0.0)
                full = full.astype(BF)
                for core in range(2):
                    for lo in range(2):
                        parts[core, t, y, lo, hi] = full[
                            lo * width : (lo + 1) * width, core * width : (core + 1) * width
                        ]
            out.copy(parts.at[1 - at.core, t, y], pair_buf.at[t, y], pair_sems.at[t, y], "core")

    def z_start(t):
        z_far[t] = share(t, z_of(half)).astype(BF)
        out.copy(z_far.at[t], z_buf.at[t, 0, t], z_sems.at[t, 0, t], "z" + marks[t])

    def chip(t, y):
        return wide(parts[at.core, t, y]) + wide(pair_buf[t, y])

    def paired(t, y):
        out.arrived(pair_buf.at[t, y], pair_sems.at[t, y])

    def y_start(t):
        y = y_of(half)
        paired(t, y)
        y_far[t] = chip(t, y).astype(BF)
        for d in range(2):
            out.copy(y_far.at[t, d], y_buf.at[d, 0, t, d], y_sems.at[d, 0, t], "y" + marks[d])

    def y_hop(step, d, t):
        y = y_of(signs[d] * (half - step))
        paired(t, y)
        value = chip(t, y)
        slot = y_buf.at[d, step - 1, t]
        if step == 1:
            out.arrived(slot.at[d], y_sems.at[d, 0, t])
            slot[d] = (value[d] + wide(slot[d])).astype(BF)
            slot[1 - d] = value[1 - d].astype(BF)
        else:
            out.arrived(slot, y_sems.at[d, step - 1, t])
            slot[...] = (value + wide(slot[...])).astype(BF)
        out.copy(slot, y_buf.at[d, step, t], y_sems.at[d, step, t], "y" + marks[d])

    def z_hop(step, d, t):
        value = share(t, z_of(signs[d] * (half - step)))
        slot = z_buf.at[d, step - 1, t]
        if step > 1 or t == d:
            out.arrived(slot, z_sems.at[d, step - 1, t])
            value = value + wide(slot[...])
        slot[...] = value.astype(BF)
        out.copy(slot, z_buf.at[d, step, t], z_sems.at[d, step, t], "z" + marks[d])

    out.arrived(theirs.at[0], swap_sems.at[0])
    for j in range(2):
        h = hid[j] + wide(theirs[0, j])
        s = jax.nn.sigmoid(h)
        act[j] = (h * s).astype(BF)
        hid[j] = s * (1.0 + h * (1.0 - s))
    z_start(1)
    make(0)
    y_start(0)
    out.arrived(theirs.at[1], swap_sems.at[1])
    for j in range(2):
        gh[j] = ((gact[j] + wide(theirs[1, j])) * hid[j]).astype(BF)
    z_start(0)
    z_hop(1, 0, 1)
    make(1)
    y_start(1)
    for step in range(1, half):
        for t in range(2):
            for d in range(2):
                y_hop(step, d, t)
            for d in range(2):
                if (step, d, t) != (1, 0, 0):
                    z_hop(step, d, 1 - t)

    for t in range(2):
        paired(t, at.y)
    own = [share(t, at.z) for t in range(2)]
    for t in range(2):
        for d in range(2):
            out.arrived(y_buf.at[d, half - 1, t], y_sems.at[d, half - 1, t])

    def y_total(t, lo, hi):
        value = wide(parts[at.core, t, at.y, lo, hi]) + wide(pair_buf[t, at.y, lo, hi])
        return value + wide(y_buf[0, half - 1, t, lo, hi]) + wide(y_buf[1, half - 1, t, lo, hi])

    ends = (("hi", at.lo, 1 - at.hi), ("diag", 1 - at.lo, 1 - at.hi), ("lo", 1 - at.lo, at.hi))
    for n, (peer, lo, hi) in enumerate(ends):
        for t in range(2):
            end_sum[n, t] = y_total(t, lo, hi).astype(BF)
        out.copy(end_sum.at[n], end_buf.at[n], end_sems.at[n], peer)
    for t, result in enumerate((grad_in, grad_out)):
        value = own[t]
        for d in range(2):
            slot = z_buf.at[d, half - 1, t]
            out.arrived(slot, z_sems.at[d, half - 1, t])
            value = value + wide(slot[...])
        result[...] = value.astype(BF)
    for n in range(3):
        out.arrived(end_buf.at[n], end_sems.at[n])
    for t, result in enumerate((layer, grad_tokens)):
        total = y_total(t, at.lo, at.hi)
        for n in range(3):
            total = total + wide(end_buf[n, t])
        result[...] = total.astype(BF)
    out.drain()


def whole(in_codes, out_codes, tokens, upstream, wi, wo):
    vmem, smem = pl.BlockSpec(memory_space=pltpu.VMEM), pl.BlockSpec(memory_space=pltpu.SMEM)
    tile, block = wi.shape, tokens.shape
    half = RING // 2
    pair = (2, 2 * block[0], tile[1])
    chunk = (2, 2, *block)
    dma = pltpu.SemaphoreType.DMA
    return pl.pallas_call(
        whole_kernel,
        name="whole_layer",
        out_shape=tuple(jax.ShapeDtypeStruct(shape, BF) for shape in (block, block, tile, tile)),
        in_specs=[smem, smem] + [pl.BlockSpec(memory_space=pl.ANY)] * 4,
        out_specs=(vmem,) * 4,
        scratch_shapes=[
            pltpu.VMEM((2, 4 * RING, 2, *block), BF),
            pltpu.VMEM((RING, *tile), BF),
            pltpu.VMEM((RING, *tile), BF),
            pltpu.VMEM(pair, F32),
            pltpu.VMEM(pair, F32),
            pltpu.VMEM((2, *pair), BF),
            pltpu.VMEM((2, *pair), BF),
            pltpu.VMEM(pair, BF),
            pltpu.VMEM(pair, BF),
            pltpu.SMEM((2, 4 * RING), jnp.int32),
            pltpu.VMEM((2, 2, RING, *chunk), BF),
            pltpu.VMEM((2, RING, *chunk), BF),
            pltpu.VMEM((2, *chunk), BF),
            pltpu.VMEM((2, half, 2, *chunk), BF),
            pltpu.VMEM((2, *tile), BF),
            pltpu.VMEM((2, half, 2, *tile), BF),
            pltpu.VMEM((3, 2, *block), BF),
            pltpu.VMEM((3, 2, *block), BF),
            dma((SENDS,)),
            dma((2, 4 * RING)),
            dma((2, RING)),
            dma((4,)),
            dma((2,)),
            dma((2, RING)),
            dma((2, half, 2)),
            dma((2, half, 2)),
            dma((3,)),
        ],
        compiler_params=pltpu.CompilerParams(
            collective_id=0, has_side_effects=True, vmem_limit_bytes=61 << 20
        ),
    )(in_codes, out_codes, tokens, upstream, wi, wo)


def per_device(tokens, upstream, w_in, in_codes, w_out, out_codes):
    layer, grad_tokens, grad_in, grad_out = whole(
        in_codes[0], out_codes[0], tokens, upstream, w_in[0, 0], w_out[0, 0]
    )
    return layer, grad_tokens, grad_in[None, None], grad_out[None, None]


def solution(mesh):
    placed = (
        P("row", "col"),
        P("row", "col"),
        P("col", "row", None, None),
        P("col", None),
        P("col", "row", None, None),
        P("col", None),
    )
    return jax.shard_map(
        per_device,
        mesh=mesh,
        in_specs=placed,
        out_specs=(
            P("row", "col"),
            P("row", "col"),
            P("col", "row", None, None),
            P("col", "row", None, None),
        ),
        check_vma=False,
    )
```

time: 106 us -> 91.1 us (0.86)
  Pallas kernels: 97.7 us -> 85.8 us
  local copies, waits for them, and re-layouts: 7.12 us -> 4.39 us
    pallas_call x4 -> x1, Pallas kernels: 97.7 us -> 85.8 us  [whole(): pl.pallas_call(whole_kernel, name='whole_layer', out_shape=tuple((jax.Sha...]
    unnamed x20 -> x8, local copies, waits for them, and re-layouts: 7.12 us -> 4.39 us
where the time goes in v5:
time: 91.1 us; the launch traced here: 90.9 us
  Pallas kernels  85.8 us (94%)
  local copies, waits for them, and re-layouts  4.39 us (5%)
    pallas_call x1, Pallas kernels, whole(): pl.pallas_call(whole_kernel, name='whole_layer', out_shape=tuple((jax.Sha...  85.8 us
    unnamed x8, local copies, waits for them, and re-layouts  4.39 us

profile of v5, /device:TPU:1, one launch (start us, length us, event | category | flops | bytes accessed | tf_op | source)
XLA Modules:
  0.0 90.9 jit_solution(17522405893002789706)
XLA Ops:
  0.6 85.8 %whole_layer.1 = (bf16[128,128]{1,0:T(8,128)(2,1)}, bf16[128,128]{1,0:T(8,128)(2,1)}, bf16[256,256]{1,0:T(8,128)(2,1)}, bf16[256,256]{1,0:T(8,128)(2,1)}) custom-call(s32[16]{0:T(128)} %bitcast.10, s32[16]{0:T(128)} %bitcast.11, bf16[128,128]{1,0:T(8,128)(2,1)} %tokens.1, bf16[128,128]{1,0:T(8,128)(2,1)} %upstream.1, bf16[256,256]{1,0:T(8,128)(2,1)} %bitcast.6, ...), custom_call_target="tpu_custom_call" | custom-call | tf_op jit(solution)/shard_map/whole_layer/pallas_call | solution.py:340
  86.4 0.0 copy-start.1
  86.5 1.4 %copy.14 = bf16[128,128]{1,0:T(8,128)(2,1)} copy(bf16[128,128]{1,0:T(8,128)(2,1)} %get-tuple-element.16) | data formatting | bytes 65536
  87.9 1.4 %copy.15 = bf16[128,128]{1,0:T(8,128)(2,1)} copy(bf16[128,128]{1,0:T(8,128)(2,1)} %get-tuple-element.17) | data formatting | bytes 65536
  89.2 0.0 copy-done.1
  89.2 0.0 copy-start
  89.2 0.7 copy.16
  89.9 0.3 copy-done
  90.2 0.7 copy.17
Async XLA Ops:
  86.4 2.8 %copy-start.1 = (bf16[256,256]{1,0:T(8,128)(2,1)S(1)}, bf16[256,256]{1,0:T(8,128)(2,1)}, u32[]{:S(2)}) copy-start(bf16[256,256]{1,0:T(8,128)(2,1)} %get-tuple-element.10) | copy-start | bytes 393220
  89.2 1.0 %copy-start = (bf16[256,256]{1,0:T(8,128)(2,1)S(1)}, bf16[256,256]{1,0:T(8,128)(2,1)}, u32[]{:S(2)}) copy-start(bf16[256,256]{1,0:T(8,128)(2,1)} %get-tuple-element.11) | copy-start | bytes 393220

commit v6 on v5

--- a/solution.py
+++ b/solution.py
@@ -94,7 +94,7 @@
 
 
 def whole_kernel(
-    in_codes, out_codes, tokens, upstream, wi_ref, wo_ref, layer, grad_tokens, grad_in, grad_out,
+    in_codes, out_codes, tokens, upstream, wi_ref, wo_ref, sums, grads,
     xg, wig, wog, hid, gact, mine, theirs, act, gh, slot_of,
     parts, pair_buf, y_far, y_buf, z_far, z_buf, end_sum, end_buf,
     send_sems, x_sems, w_sems, own_sems, swap_sems, pair_sems, y_sems, z_sems, end_sems,
@@ -153,7 +153,7 @@
                 continue
             t = n // 2
             for d, (sign, mark) in enumerate(flows):
-                if step == half and t != d:
+                if step == half and (t != d or t == 1):
                     continue
                 onward = step < half - 1 or (step == half - 1 and t == d)
                 w_pass(t, lax.rem(at.z + sign * step + RING, RING), *(("z" + mark,) if onward else ()))
@@ -179,6 +179,7 @@
         out.copy(mine.at[which], theirs.at[which], swap_sems.at[which], "lo")
 
     inward(in_codes, 0, wig, hid, ((1,), (0,)))
+    w_pass(1, lax.rem(at.z + half, RING))
     inward(out_codes, 1, wog, gact, ((1,), (1,)))
 
     def slot_at(code, _):
@@ -313,20 +314,20 @@
         for t in range(2):
             end_sum[n, t] = y_total(t, lo, hi).astype(BF)
         out.copy(end_sum.at[n], end_buf.at[n], end_sems.at[n], peer)
-    for t, result in enumerate((grad_in, grad_out)):
+    for t in range(2):
         value = own[t]
         for d in range(2):
             slot = z_buf.at[d, half - 1, t]
             out.arrived(slot, z_sems.at[d, half - 1, t])
             value = value + wide(slot[...])
-        result[...] = value.astype(BF)
+        grads[t] = value.astype(BF)
     for n in range(3):
         out.arrived(end_buf.at[n], end_sems.at[n])
-    for t, result in enumerate((layer, grad_tokens)):
+    for t in range(2):
         total = y_total(t, at.lo, at.hi)
         for n in range(3):
             total = total + wide(end_buf[n, t])
-        result[...] = total.astype(BF)
+        sums[t] = total.astype(BF)
     out.drain()
 
 
@@ -340,9 +341,9 @@
     return pl.pallas_call(
         whole_kernel,
         name="whole_layer",
-        out_shape=tuple(jax.ShapeDtypeStruct(shape, BF) for shape in (block, block, tile, tile)),
+        out_shape=tuple(jax.ShapeDtypeStruct(shape, BF) for shape in ((2, *block), (2, *tile))),
         in_specs=[smem, smem] + [pl.BlockSpec(memory_space=pl.ANY)] * 4,
-        out_specs=(vmem,) * 4,
+        out_specs=(vmem,) * 2,
         scratch_shapes=[
             pltpu.VMEM((2, 4 * RING, 2, *block), BF),
             pltpu.VMEM((RING, *tile), BF),
@@ -379,10 +380,10 @@
 
 
 def per_device(tokens, upstream, w_in, in_codes, w_out, out_codes):
-    layer, grad_tokens, grad_in, grad_out = whole(
+    sums, grads = whole(
         in_codes[0], out_codes[0], tokens, upstream, w_in[0, 0], w_out[0, 0]
     )
-    return layer, grad_tokens, grad_in[None, None], grad_out[None, None]
+    return sums[0], sums[1], grads[0][None, None], grads[1][None, None]
 
 
 def solution(mesh):

time: 91.1 us -> 89.8 us (0.986)
  local copies, waits for them, and re-layouts: 4.39 us -> 3.09 us
    unnamed x8 -> x0, local copies, waits for them, and re-layouts: 4.39 us -> none
    another operation x0 -> x1, local copies, waits for them, and re-layouts: none -> 1.68 us  [per_device(): return (sums[0], sums[1], grads[0][None, None], grads[1][None, None])]
    squeeze x0 -> x1, local copies, waits for them, and re-layouts: none -> 1.4 us  [per_device(): return (sums[0], sums[1], grads[0][None, None], grads[1][None, None])]
where the time goes in v6:
time: 89.8 us; the launch traced here: 89.6 us
  Pallas kernels  85.8 us (96%)
  local copies, waits for them, and re-layouts  3.09 us (3%)
    pallas_call x1, Pallas kernels, whole(): pl.pallas_call(whole_kernel, name='whole_layer', out_shape=tuple((jax.Sha...  85.8 us

profile of v6, /device:TPU:1, one launch (start us, length us, event | category | flops | bytes accessed | tf_op | source)
XLA Modules:
  0.0 89.6 jit_solution(5033079229933540682)
XLA Ops:
  0.6 85.8 %whole_layer.1 = (bf16[2,128,128]{2,1,0:T(8,128)(2,1)}, bf16[2,256,256]{2,1,0:T(8,128)(2,1)}) custom-call(s32[16]{0:T(128)} %bitcast.14, s32[16]{0:T(128)} %bitcast.15, bf16[128,128]{1,0:T(8,128)(2,1)} %tokens.1, bf16[128,128]{1,0:T(8,128)(2,1)} %upstream.1, bf16[256,256]{1,0:T(8,128)(2,1)} %bitcast.12, bf16[256,256]{1,0:T(8,128)(2,1)} %bitcast.13), custom_call_target="tpu_custom_call" | custom-call | tf_op jit(solution)/shard_map/whole_layer/pallas_call | solution.py:341
  86.5 1.4 %slice_bitcast_fusion.2 = (bf16[128,128]{1,0:T(8,128)(2,1)}, bf16[128,128]{1,0:T(8,128)(2,1)}) fusion(bf16[2,128,128]{2,1,0:T(8,128)(2,1)} %get-tuple-element.6), kind=kLoop, calls=%fused_computation.2 | loop fusion | bytes 131072 | tf_op jit(solution)/shard_map/squeeze | solution.py:386
  87.9 1.7 %slice_bitcast_fusion = (bf16[1,1,256,256]{3,2,1,0:T(8,128)(2,1)}, bf16[1,1,256,256]{3,2,1,0:T(8,128)(2,1)}) fusion(bf16[2,256,256]{2,1,0:T(8,128)(2,1)} %get-tuple-element.7), kind=kLoop, calls=%fused_computation | loop fusion | bytes 524288 | tf_op jit(solution)/shard_map/broadcast_in_dim;squeeze | solution.py:386
